TPU v7x, 512 devices: a whole 4x4x16 slice. The times are simulated.
512 devices in a mesh: mol: 128 (over z, y, core), traj: 4 (over x).
Axes of the slice: x: 4, y: 4, z: 16, core: 2. Of those that a mesh axis runs over, the one named last changes fastest.
Arguments:
- positions: float32 [64, 16384], P('traj', 'mol'), parts along dimension 0, may hold values from -1.2 to 1.2
- velocities: float32 [64, 16384], P('traj', 'mol'), parts along dimension 0, may hold values from -3 to 3
- amplitudes: float32 [4096, 64], P('mol', 'traj'), parts along dimension 1, may hold values from -6 to 6
- momenta: float32 [4096, 64], P('mol', 'traj'), parts along dimension 1, may hold values from -6 to 6
- sites: int32 [16384], P('mol'), may hold values from 0 to 32767
- wavevectors: int32 [4096], replicated, may hold values from 1 to 32767
- mode_freq: float32 [4096], P('mol'), may hold values from 0.5 to 2
- coupling: float32 [4096], P('mol'), may hold values from 0.0078125 to 0.03125
- depth: float32 [16384], P('mol'), may hold values from 0.5 to 2
- stiffness: float32 [16384], P('mol'), may hold values from 0.8 to 1.5
- dipole_slope: float32 [16384], P('mol'), may hold values from -4 to 4
Outputs:
- final_positions: float32 [64, 16384], P('traj', 'mol'), parts along dimension 0
- final_velocities: float32 [64, 16384], P('traj', 'mol'), parts along dimension 0
- final_amplitudes: float32 [4096, 64], P('mol', 'traj'), parts along dimension 1
- final_momenta: float32 [4096, 64], P('mol', 'traj'), parts along dimension 1
There are 4 independent parts, one for each index of `traj`. A program takes and returns all parts, laid end to end along the dimension named above; an argument that names none is the same for every part. Nothing has to cross between parts.
All inputs are finite; a program needn't handle non-finite values.
Results may differ from a plain program's by a relative error of at most 0.0003.
Values sent between devices are 32-bit elements; how exact they have to be, the bound alone decides.
No kernel may reach another device: no remote copies, remote signals or barrier semaphores. Data moves between devices by JAX's collectives and lax.ppermute only.
A program may use at most 64 MiB of HBM per device.

v0:
```python
import math

import jax
import jax.numpy as jnp
from jax import lax
from jax.sharding import PartitionSpec as P

STEPS = 2


def phase_tile(waves, sites, lattice):
    high = sites // 256
    low = sites % 256
    first = waves[:, None] * high[None, :] % lattice
    residue = (first * 256 + waves[:, None] * low[None, :]) % lattice
    angle = residue.astype(jnp.float32) * (2.0 * math.pi / lattice)
    return jnp.sin(angle)


def project_dipole(tile, dipole):
    return lax.dot_general(
        tile,
        dipole,
        (((1,), (1,)), ((), ())),
        precision=lax.Precision.HIGHEST,
        preferred_element_type=jnp.float32,
    )


def project_modes(weighted, tile):
    return lax.dot_general(
        weighted,
        tile,
        (((0,), (0,)), ((), ())),
        precision=lax.Precision.HIGHEST,
        preferred_element_type=jnp.float32,
    )


def advance_bonds(positions, velocities, pull, depth, stiffness, dipole_slope, step_time):
    damped = jnp.exp(-stiffness[None, :] * positions)
    force = (
        -2.0 * depth[None, :] * stiffness[None, :] * (1.0 - damped) * damped
        - dipole_slope[None, :] * pull
    )
    velocities = velocities + step_time * force
    positions = positions + step_time * velocities
    return (positions, velocities)


def local(
    positions,
    velocities,
    amplitudes,
    momenta,
    sites,
    wavevectors,
    mode_freq,
    coupling,
    depth,
    stiffness,
    dipole_slope,
):
    step_time = 0.2
    lattice = 2 * sites.shape[0] * lax.axis_size("mol")
    owned_rows = amplitudes.shape[0]
    stored = phase_tile(wavevectors, sites, lattice)

    def tile_rows():
        return stored

    for step in range(STEPS):
        dipole = dipole_slope[None, :] * positions

        def drive_term(start, count, dipole=dipole):
            return project_dipole(tile_rows(), dipole)

        drive = lax.psum_scatter(
            drive_term(jnp.int32(0), lax.axis_size("mol") * owned_rows),
            "mol",
            scatter_dimension=0,
            tiled=True,
        )
        momenta = momenta + step_time * (
            -(mode_freq * mode_freq)[:, None] * amplitudes - coupling[:, None] * drive
        )
        amplitudes = amplitudes + step_time * momenta
        weighted = coupling[:, None] * amplitudes
        pull = project_modes(lax.all_gather(weighted, "mol", axis=0, tiled=True), tile_rows())
        positions, velocities = advance_bonds(
            positions, velocities, pull, depth, stiffness, dipole_slope, step_time
        )
    return (positions, velocities, amplitudes, momenta)


def solution(mesh):
    return jax.shard_map(
        local,
        mesh=mesh,
        in_specs=(
            P("traj", "mol"),
            P("traj", "mol"),
            P("mol", "traj"),
            P("mol", "traj"),
            P("mol"),
            P(),
            P("mol"),
            P("mol"),
            P("mol"),
            P("mol"),
            P("mol"),
        ),
        out_specs=(P("traj", "mol"), P("traj", "mol"), P("mol", "traj"), P("mol", "traj")),
        check_vma=False,
    )
```

profile of v0, /device:TPU:1, one launch (start us, length us, event | category | flops | bytes accessed | tf_op | source)
XLA Modules:
  0.0 796.6 jit_solution(9365872709216338628)
XLA Ops:
  7.2 0.0 reduce-scatter.7.cloned.1.call-start
  7.2 0.7 and_select_fusion.1
  7.9 13.8 %fusion.17 = f32[4096,16]{1,0:T(8,128)} fusion(s32[128]{0:T(128)S(1)} %get-tuple-element.10, s32[128]{0:T(128)S(1)} %get-tuple-element.9, s32[4096]{0:T(1024)} %param.16, f32[16,128]{1,0:T(8,128)} %param.11, f32[128]{0:T(128)} %param.21), kind=kOutput, calls=%fused_computation.24 | convolution fusion | flops 115345408 | bytes 288256
  21.7 0.0 copy-start.8
  21.7 0.0 copy-start.3
  21.7 0.0 copy-start.4
  21.7 0.0 copy-start
  21.7 0.0 copy-start.1
  21.7 0.0 copy-start.2
  21.7 0.0 reduce-scatter.7.cloned.1.call-update
  21.7 0.0 reduce-scatter.9.cloned.1.call-start
  21.8 0.5 copy-done.8
  22.3 0.0 copy-done.3
  22.3 0.0 copy-done.4
  22.3 257.0 %reduce-scatter.7.cloned.1.call-done = f32[32,16]{1,0:T(8,128)} async-done(((f32[4096,16]{1,0:T(8,128)}), f32[32,16]{1,0:T(8,128)}) %reduce-scatter.7.cloned.1.call-update) | async-done | bytes 2064
  279.3 0.8 copy.20
  280.1 0.0 copy-done
  280.1 0.0 copy-done.1
  280.1 0.0 copy-done.2
  280.1 0.0 copy-start.5
  280.2 0.0 copy-start.6
  280.2 0.0 copy-start.7
  280.2 0.0 copy-start.9
  280.2 111.7 %all-gather = f32[128,32,16]{1,2,0:T(8,128)S(1)} all-gather(f32[1,32,16]{1,2,0:T(8,128)S(1)} %multiply_bitcast_fusion.1), channel_id=1, replica_groups=mesh['mol'=128,'traj'=4] {'mol'}, dimensions={0}, use_global_device_ids=true | all-gather | bytes 264192 | tf_op jit(solution)/shard_map/all_gather | solution.py:89
  391.9 0.3 copy.17
  392.2 0.5 reshape.21
  392.7 0.0 copy-done.5
  392.7 0.0 copy-done.6
  392.8 0.0 copy-done.7
  392.8 0.0 copy-done.9
  392.8 10.0 %fusion.12 = f32[16,128]{1,0:T(8,128)S(1)} fusion(f32[16,128]{1,0:T(8,128)S(1)} %copy-done.6, f32[4096,16]{0,1:T(8,128)S(1)} %reshape.21, s32[128]{0:T(128)S(1)} %get-tuple-element.10, s32[128]{0:T(128)S(1)} %get-tuple-element.9, s32[4096]{0:T(1024)S(1)} %copy-done.5, f32[16,128]{1,0:T(8,128)S(1)} %copy-done.7, f32[128]{0:T(128)S(1)} %copy-done.9, ...), kind=kOutput, calls=%fused_computation.22 | convolution fusion | flops 115359744 | bytes 305664 | tf_op jit(solution)/shard_map/dot_general | solution.py:31
  402.8 13.3 %fusion.14 = f32[4096,16]{1,0:T(8,128)} fusion(s32[128]{0:T(128)S(1)} %get-tuple-element.10, s32[128]{0:T(128)S(1)} %get-tuple-element.9, s32[4096]{0:T(1024)S(1)} %copy-done.5, f32[128]{0:T(128)S(1)} %copy-done.9, f32[16,128]{1,0:T(8,128)S(1)} %copy-done.7, f32[16,128]{1,0:T(8,128)S(1)} %fusion.12), kind=kOutput, calls=%fused_computation.23 | convolution fusion | flops 115349504 | bytes 296448
  416.1 0.0 reduce-scatter.9.cloned.1.call-update
  416.1 249.2 %reduce-scatter.9.cloned.1.call-done = f32[32,16]{1,0:T(8,128)} async-done(((f32[4096,16]{1,0:T(8,128)}), f32[32,16]{1,0:T(8,128)}) %reduce-scatter.9.cloned.1.call-update) | async-done | bytes 2064
  665.3 0.8 copy.22
  666.1 0.6 multiply_bitcast_fusion
  666.7 111.6 %all-gather.1 = f32[128,32,16]{1,2,0:T(8,128)S(1)} all-gather(f32[1,32,16]{1,2,0:T(8,128)S(1)} %get-tuple-element.4), channel_id=1, replica_groups=mesh['mol'=128,'traj'=4] {'mol'}, dimensions={0}, use_global_device_ids=true | all-gather | bytes 264192 | tf_op jit(solution)/shard_map/all_gather | solution.py:89
  778.2 0.3 copy.18
  778.6 0.5 reshape.23
  779.1 10.7 %multiply_add_fusion = (f32[16,128]{1,0:T(8,128)}, f32[16,128]{1,0:T(8,128)}) fusion(f32[16,128]{1,0:T(8,128)S(1)} %copy-done.7, f32[16,128]{1,0:T(8,128)S(1)} %fusion.12, f32[4096,16]{0,1:T(8,128)S(1)} %reshape.23, s32[128]{0:T(128)S(1)} %get-tuple-element.10, s32[128]{0:T(128)S(1)} %get-tuple-element.9, s32[4096]{0:T(1024)S(1)} %copy-done.5, ...), kind=kOutput, calls=%fused_computation.25 | convolution fusion | flops 115367936 | bytes 313856 | tf_op jit(solution)/shard_map/dot_general | solution.py:31
  (3 shorter events, 0.0 us)
Async XLA Ops:
  7.2 272.2 %reduce-scatter.7.cloned.1.call-start = ((), (), s32[]{:S(2)}) async-start(), calls=%async_computation.2 | async-start | bytes 2113536
  21.7 0.7 copy-start.8
  21.7 0.7 copy-start.3
  21.7 0.7 copy-start.4
  21.7 258.5 %copy-start = (f32[32,16]{0,1:T(8,128)S(1)}, f32[32,16]{0,1:T(8,128)}, u32[]{:S(2)}) copy-start(f32[32,16]{0,1:T(8,128)} %param.13) | copy-start | bytes 6148
  21.7 258.4 %copy-start.1 = (f32[32,16]{0,1:T(8,128)S(1)}, f32[32,16]{0,1:T(8,128)}, u32[]{:S(2)}) copy-start(f32[32,16]{0,1:T(8,128)} %param.14) | copy-start | bytes 6148
  21.7 258.4 %copy-start.2 = (f32[32]{0:T(128)S(1)}, f32[32]{0:T(128)}, u32[]{:S(2)}) copy-start(f32[32]{0:T(128)} %param.18) | copy-start | bytes 388
  21.7 643.5 %reduce-scatter.9.cloned.1.call-start = ((), (), s32[]{:S(2)}) async-start(), calls=%async_computation.3 | async-start | bytes 2113536
  280.1 112.6 %copy-start.5 = (s32[4096]{0:T(1024)S(1)}, s32[4096]{0:T(1024)}, u32[]{:S(2)}) copy-start(s32[4096]{0:T(1024)} %param.16) | copy-start | bytes 49156
  280.2 112.6 %copy-start.6 = (f32[16,128]{1,0:T(8,128)S(1)}, f32[16,128]{1,0:T(8,128)}, u32[]{:S(2)}) copy-start(f32[16,128]{1,0:T(8,128)} %param.12) | copy-start | bytes 24580
  280.2 112.6 %copy-start.7 = (f32[16,128]{1,0:T(8,128)S(1)}, f32[16,128]{1,0:T(8,128)}, u32[]{:S(2)}) copy-start(f32[16,128]{1,0:T(8,128)} %param.11) | copy-start | bytes 24580
  280.2 112.6 %copy-start.9 = (f32[128]{0:T(128)S(1)}, f32[128]{0:T(128)}, u32[]{:S(2)}) copy-start(f32[128]{0:T(128)} %param.21) | copy-start | bytes 1540
Sparse Core Ops, SparseCore 0:
  21.8 257.4 reduce-scatter.6
  416.2 248.9 reduce-scatter.8
where the time goes:
time: 797 us
  waiting for transfers between devices  506 us (63%)
  blocking collectives  223 us (28%)
  matrix products  47.8 us (6%)
  between operations  14.2 us (2%)
    unnamed x4, waiting for transfers between devices  506 us
    all_gather x2, blocking collectives, local(): lax.all_gather(weighted, 'mol', axis=0, tiled=True)  223 us
    unnamed x2, matrix products  27 us
    dot_general x2, matrix products, project_modes(): lax.dot_general(weighted, tile, (((0,), (0,)), ((), ())), precision=lax.P...  20.8 us
  transfers between devices with their start and end apart: 2, of which 2 were waited for; matrix products, arithmetic and copies ran while one was open for 0% of the time, Pallas kernels for 0%

commit v1 on v0

v1 whole, which is shorter than its diff:
```python
import functools

import jax
import jax.numpy as jnp
from jax import lax
from jax.experimental import pallas as pl
from jax.experimental.pallas import tpu as pltpu
from jax.sharding import PartitionSpec as P

STEP_TIME = 0.2
SINE = (25.132741928100586, -64.83582305908203, 67.0767593383789, -38.49842071533203, 14.06550407409668, -3.1933720111846924)
LANES = 128
F32, BF16 = jnp.float32, jnp.bfloat16


def split(x):
    high = x.astype(BF16)
    return high, (x - high.astype(F32)).astype(BF16)


def dot(a, b):
    return lax.dot_general(a, b, (((1,), (0,)), ((), ())), preferred_element_type=F32)


def sine_of(product, shift):
    turn = (product << shift).astype(F32) * (2.0**-32)
    square = turn * turn
    value = jnp.full_like(square, SINE[-1])
    for factor in SINE[-2::-1]:
        value = value * square + factor
    return turn * (0.25 - square) * value


def lane_groups(shape, width):
    return lax.broadcasted_iota(jnp.int32, shape, len(shape) - 1) // width


def block_diagonal(dipole, out_ref):
    traj, mols = dipole.shape
    pack = LANES // traj
    across = jnp.concatenate([dipole] * pack, axis=0).T
    high, low = split(across)
    high, low = high.astype(F32), low.astype(F32)
    group = lane_groups((mols, LANES), traj)
    for place in range(pack):
        rows = pl.ds(place * mols, mols)
        out_ref[rows, :LANES] = jnp.where(group == place, high, 0.0).astype(BF16)
        out_ref[rows, LANES:] = jnp.where(group == place, low, 0.0).astype(BF16)


def drive_rows(high_ref, low_ref, spread_ref):
    both = dot(high_ref[...], spread_ref[...])
    return both[:, :LANES] + both[:, LANES:] + dot(low_ref[...], spread_ref[:, :LANES])


def pull_of(rows_ref, high_ref, low_ref, traj, mols):
    high, low = split(rows_ref[...].T)
    pack = LANES // traj
    total = None
    for pair in range(pack // 2):
        rows = slice(pair * 2 * traj, (pair + 1) * 2 * traj)
        columns = pl.ds(pair * 2 * mols, 2 * mols)
        left = jnp.concatenate([high[rows], low[rows]], axis=0)
        first = dot(left, high_ref[:, columns])
        second = dot(high[rows], low_ref[:, columns])
        for side in range(2):
            cols = slice(side * mols, (side + 1) * mols)
            at = side * traj
            part = first[at : at + traj, cols] + first[2 * traj + at : 2 * traj + at + traj, cols] + second[at : at + traj, cols]
            total = part if total is None else total + part
    return total


def advance_bonds(positions, velocities, pull, depth, stiffness, dipole_slope):
    damped = jnp.exp(-stiffness * positions)
    force = -2.0 * depth * stiffness * (1.0 - damped) * damped - dipole_slope * pull
    velocities = velocities + STEP_TIME * force
    return positions + STEP_TIME * velocities, velocities


def first_kernel(shift, positions, slope, sites, waves, high_ref, low_ref, partial_ref, spread_ref):
    block_diagonal(slope[...] * positions[...], spread_ref)
    mols = sites.shape[1]
    pack = waves.shape[1]
    total = None
    for pair in range(pack // 2):
        for place in (2 * pair, 2 * pair + 1):
            columns = pl.ds(place * mols, mols)
            high, low = split(sine_of(waves[:, place : place + 1] * sites[...], shift))
            high_ref[:, columns] = high
            low_ref[:, columns] = low
        columns = pl.ds(2 * pair * mols, 2 * mols)
        both = dot(high_ref[:, columns], spread_ref[columns, :])
        part = both[:, :LANES] + both[:, LANES:] + dot(low_ref[:, columns], spread_ref[columns, :LANES])
        total = part if total is None else total + part
    partial_ref[...] = total


def pack_rows(block, traj):
    rows = block.shape[0]
    pack = LANES // traj
    wide = jnp.concatenate([block] * pack, axis=1)
    place = lax.broadcasted_iota(jnp.int32, wide.shape, 0) % pack
    wide = jnp.where(lane_groups(wide.shape, traj) == place, wide, 0.0)
    return wide.reshape(rows // pack, pack, LANES).sum(axis=1)


def unpack_rows(packed, traj):
    rows = packed.shape[0]
    pack = LANES // traj
    wide = jnp.broadcast_to(packed[:, None, :], (rows, pack, LANES)).reshape(rows * pack, LANES)
    place = lax.broadcasted_iota(jnp.int32, wide.shape, 0) % pack
    wide = jnp.where(lane_groups(wide.shape, traj) == place, wide, 0.0)
    total = wide[:, :traj]
    for group in range(1, pack):
        total = total + wide[:, group * traj : (group + 1) * traj]
    return total


def column_of(row, traj):
    modes = row.shape[1]
    spread = jnp.broadcast_to(row, (modes, modes))
    own = lax.broadcasted_iota(jnp.int32, (modes, modes), 0) == lax.broadcasted_iota(jnp.int32, (modes, modes), 1)
    return jnp.broadcast_to(jnp.where(own, spread, 0.0).sum(axis=1, keepdims=True), (modes, traj))


def modes_kernel(received, amplitudes, momenta, freq, coupling, amplitudes_out, momenta_out, weighted_ref):
    traj = amplitudes.shape[1]
    rows = amplitudes.shape[0] * traj // LANES
    pair = received[...].reshape(-1, 2 * rows, LANES).sum(axis=0)
    drive = unpack_rows(pair[:rows] + pair[rows:], traj)
    freq_of = column_of(freq[...], traj)
    coupling_of = column_of(coupling[...], traj)
    new_momenta = momenta[...] + STEP_TIME * (-(freq_of * freq_of) * amplitudes[...] - coupling_of * drive)
    new_amplitudes = amplitudes[...] + STEP_TIME * new_momenta
    momenta_out[...] = new_momenta
    amplitudes_out[...] = new_amplitudes
    weighted = pack_rows(coupling_of * new_amplitudes, traj)
    twice = jnp.concatenate([weighted, weighted], axis=0)
    copies = weighted_ref.shape[0] // (2 * rows)
    weighted_ref[...] = jnp.broadcast_to(twice[None], (copies, 2 * rows, LANES)).reshape(weighted_ref.shape)


def middle_kernel(rows, high_ref, low_ref, positions, velocities, depth, stiffness, slope, positions_out, velocities_out, partial_ref, spread_ref):
    pull = pull_of(rows, high_ref, low_ref, *positions.shape)
    new_positions, new_velocities = advance_bonds(
        positions[...], velocities[...], pull, depth[...], stiffness[...], slope[...]
    )
    positions_out[...] = new_positions
    velocities_out[...] = new_velocities
    block_diagonal(slope[...] * new_positions, spread_ref)
    partial_ref[...] = drive_rows(high_ref, low_ref, spread_ref)


def last_kernel(rows, high_ref, low_ref, positions, velocities, depth, stiffness, slope, positions_out, velocities_out):
    pull = pull_of(rows, high_ref, low_ref, *positions.shape)
    new_positions, new_velocities = advance_bonds(
        positions[...], velocities[...], pull, depth[...], stiffness[...], slope[...]
    )
    positions_out[...] = new_positions
    velocities_out[...] = new_velocities


def call(kernel, outs, name, scratch=(), interpret=False):
    return pl.pallas_call(
        kernel,
        out_shape=[jax.ShapeDtypeStruct(shape, dtype) for shape, dtype in outs],
        scratch_shapes=list(scratch),
        name=name,
        interpret=interpret,
        compiler_params=None if interpret else pltpu.CompilerParams(vmem_limit_bytes=48 << 20),
    )


def stages(traj, mols, modes, owned, shift, interpret=False):
    pack = LANES // traj
    rows = modes // pack
    phase = ((rows, pack * mols), BF16)
    packed = ((rows, LANES), F32)
    bonds = ((traj, mols), F32)
    own = ((owned, traj), F32)
    spread = [pltpu.VMEM((pack * mols, 2 * LANES), BF16)]
    first = call(functools.partial(first_kernel, shift), [phase, phase, packed], "first", spread, interpret)
    update = call(modes_kernel, [own, own, packed], "modes", (), interpret)
    middle = call(middle_kernel, [bonds, bonds, packed], "middle", spread, interpret)
    last = call(last_kernel, [bonds, bonds], "last", (), interpret)
    return first, update, middle, last


def exchange(packed, devices):
    blocks = packed.reshape(devices, -1, LANES)
    return lax.all_to_all(blocks, "mol", 0, 0, tiled=True).reshape(packed.shape)


def local(positions, velocities, amplitudes, momenta, sites, wavevectors, mode_freq, coupling, depth, stiffness, dipole_slope):
    devices = lax.axis_size("mol")
    traj, mols = positions.shape
    lattice = 2 * mols * devices
    first, update, middle, last = stages(traj, mols, wavevectors.shape[0], amplitudes.shape[0], 33 - lattice.bit_length())
    row = lambda x: x.reshape(1, -1)
    depth, stiffness, slope = row(depth), row(stiffness), row(dipole_slope)
    freq, coupling = row(mode_freq), row(coupling)
    high, low, partial = first(positions, slope, row(sites), wavevectors.reshape(-1, LANES // traj))
    amplitudes, momenta, weighted = update(exchange(partial, devices), amplitudes, momenta, freq, coupling)
    rows = exchange(weighted, devices)
    positions, velocities, partial = middle(rows, high, low, positions, velocities, depth, stiffness, slope)
    amplitudes, momenta, weighted = update(exchange(partial, devices), amplitudes, momenta, freq, coupling)
    rows = exchange(weighted, devices)
    positions, velocities = last(rows, high, low, positions, velocities, depth, stiffness, slope)
    return positions, velocities, amplitudes, momenta


def solution(mesh):
    both, mode, mol = P("traj", "mol"), P("mol", "traj"), P("mol")
    return jax.shard_map(
        local,
        mesh=mesh,
        in_specs=(both, both, mode, mode, mol, P(), mol, mol, mol, mol, mol),
        out_specs=(both, both, mode, mode),
        check_vma=False,
    )
```

time: 797 us -> 139 us (0.17)
  waiting for transfers between devices: 506 us -> 38.8 us
  blocking collectives: 223 us -> 57.1 us
  matrix products: 47.8 us -> 0 us
  starting transfers between devices: 0.08 us -> 29 us
  between operations: 14.2 us -> 0.73 us
    unnamed x4 -> x0, waiting for transfers between devices: 506 us -> none
    all_gather x2 -> x0, blocking collectives: 223 us -> none  [local(): lax.all_gather(weighted, 'mol', axis=0, tiled=True)]
    all_to_all x0 -> x2, blocking collectives: none -> 57.1 us  [exchange(): return lax.all_to_all(blocks, 'mol', 0, 0, tiled=True).reshape(packed.shape)]
    all_to_all x0 -> x2, waiting for transfers between devices: none -> 38.8 us  [exchange(): return lax.all_to_all(blocks, 'mol', 0, 0, tiled=True).reshape(packed.shape)]
    all_to_all x0 -> x2, starting transfers between devices: none -> 29 us  [exchange(): return lax.all_to_all(blocks, 'mol', 0, 0, tiled=True).reshape(packed.shape)]
    unnamed x2 -> x0, matrix products: 27 us -> none
    dot_general x2 -> x0, matrix products: 20.8 us -> none  [project_modes(): lax.dot_general(weighted, tile, (((0,), (0,)), ((), ())), precision=lax.P...]
  transfers between devices with their start and end apart: 2 -> 2, of which waited for: 2 -> 2; matrix products, arithmetic and copies ran while one was open for 0% -> 1% of each run, Pallas kernels for 0% -> 0%
where the time goes in v1:
time: 139 us; the launch traced here: 137 us
  blocking collectives  57.1 us (41%)
  waiting for transfers between devices  38.8 us (28%)
  starting transfers between devices  29 us (21%)
  Pallas kernels  6.55 us (5%)
  local copies, waits for them, and re-layouts  5.01 us (4%)
    all_to_all x2, blocking collectives, exchange(): return lax.all_to_all(blocks, 'mol', 0, 0, tiled=True).reshape(packed.shape)  57.1 us
    all_to_all x2, waiting for transfers between devices, exchange(): return lax.all_to_all(blocks, 'mol', 0, 0, tiled=True).reshape(packed.shape)  38.8 us
    all_to_all x2, starting transfers between devices, exchange(): return lax.all_to_all(blocks, 'mol', 0, 0, tiled=True).reshape(packed.shape)  29 us
    unnamed x24, local copies, waits for them, and re-layouts  4.13 us
  transfers between devices with their start and end apart: 2, of which 2 were waited for; matrix products, arithmetic and copies ran while one was open for 1% of the time, Pallas kernels for 0%

profile of v1, /device:TPU:1, one launch (start us, length us, event | category | flops | bytes accessed | tf_op | source)
XLA Modules:
  0.0 137.2 jit_solution(5981935557652865489)
XLA Ops:
  0.6 0.0 copy-start
  0.6 0.9 reshape.55.waves
  1.5 0.0 copy-start.2
  1.5 0.0 copy-start.7
  1.6 0.0 copy-done
  1.6 0.6 copy-done.2
  2.2 0.0 copy-done.7
  2.2 2.8 %first.1 = (bf16[512,1024]{1,0:T(8,128)(2,1)S(1)}, bf16[512,1024]{1,0:T(8,128)(2,1)S(1)}, f32[512,128]{1,0:T(8,128)}) custom-call(f32[16,128]{1,0:T(8,128)S(1)} %copy-done, f32[1,128]{1,0:T(1,128)S(1)} %bitcast.20, s32[1,128]{1,0:T(1,128)S(1)} %bitcast.31, s32[512,8]{1,0:T(8,128)S(1)} %reshape.55.waves), custom_call_target="tpu_custom_call" | custom-call | tf_op jit(solution)/shard_map/first/pallas_call | solution.py:203
  5.0 0.0 copy-start.8
  5.0 20.7 %all-to-all-start = ((f32[128,4,128]{2,1,0:T(4,128)}), f32[128,4,128]{2,1,0:T(4,128)S(1)}, u32[]{:S(2)}, u32[]{:S(2)}) async-start(f32[128,4,128]{2,1,0:T(4,128)} %bitcast.2), calls=%async_computation | async-start | bytes 524288 | tf_op jit(solution)/shard_map/all_to_all | solution.py:192
  25.6 0.0 copy-done.8
  25.7 0.0 copy-start.9
  25.7 0.1 copy.19.amplitudes
  25.7 0.6 copy-done.9
  26.4 0.1 copy.20.momenta
  26.4 19.7 %all-to-all-done = f32[128,4,128]{2,1,0:T(4,128)S(1)} async-done(((f32[128,4,128]{2,1,0:T(4,128)}), f32[128,4,128]{2,1,0:T(4,128)S(1)}, u32[]{:S(2)}, u32[]{:S(2)}) %all-to-all-start) | async-done | bytes 262176 | tf_op jit(solution)/shard_map/all_to_all | solution.py:192
  46.1 0.0 copy-start.3
  46.1 0.0 copy-start.4
  46.1 0.7 copy-done.3
  46.7 0.0 copy-done.4
  46.8 0.3 modes.2
  47.1 28.6 %all_to_all.20 = f32[128,4,128]{2,1,0:T(4,128)S(1)} all-to-all(f32[128,4,128]{2,1,0:T(4,128)S(1)} %bitcast.18), channel_id=1, replica_groups=mesh['mol'=128,'traj'=4] {'mol'}, dimensions={0} | all-to-all | bytes 524288 | tf_op jit(solution)/shard_map/all_to_all | solution.py:192
  75.7 0.0 copy-start.1
  75.7 0.0 copy-start.5
  75.7 0.0 copy-start.6
  75.7 0.7 copy-done.1
  76.4 0.0 copy-done.5
  76.4 0.0 copy-done.6
  76.4 1.3 middle.1
  77.7 28.6 %all_to_all.21 = f32[128,4,128]{2,1,0:T(4,128)S(1)} all-to-all(f32[128,4,128]{2,1,0:T(4,128)S(1)} %bitcast.19), channel_id=1, replica_groups=mesh['mol'=128,'traj'=4] {'mol'}, dimensions={0} | all-to-all | bytes 524288 | tf_op jit(solution)/shard_map/all_to_all | solution.py:192
  106.3 1.1 modes.3
  107.3 8.3 %all-to-all-start.3 = ((f32[128,4,128]{2,1,0:T(4,128)}), f32[128,4,128]{2,1,0:T(4,128)S(1)}, u32[]{:S(2)}, u32[]{:S(2)}) async-start(f32[128,4,128]{2,1,0:T(4,128)} %bitcast.12), calls=%async_computation.3 | async-start | bytes 524288 | tf_op jit(solution)/shard_map/all_to_all | solution.py:192
  115.6 0.7 copy.21
  116.3 0.7 copy.22
  117.0 19.1 %all-to-all-done.3 = f32[128,4,128]{2,1,0:T(4,128)S(1)} async-done(((f32[128,4,128]{2,1,0:T(4,128)}), f32[128,4,128]{2,1,0:T(4,128)S(1)}, u32[]{:S(2)}, u32[]{:S(2)}) %all-to-all-start.3) | async-done | bytes 262176 | tf_op jit(solution)/shard_map/all_to_all | solution.py:192
  136.1 1.1 last.1
Async XLA Ops:
  0.6 0.9 copy-start
  1.5 0.7 copy-start.2
  1.5 0.7 copy-start.7
  5.0 20.7 %copy-start.8 = (f32[32,16]{0,1:T(8,128)S(1)}, f32[32,16]{0,1:T(8,128)}, u32[]{:S(2)}) copy-start(f32[32,16]{0,1:T(8,128)} %param.13) | copy-start | bytes 6148
  5.0 41.1 %all-to-all-start = ((f32[128,4,128]{2,1,0:T(4,128)}), f32[128,4,128]{2,1,0:T(4,128)S(1)}, u32[]{:S(2)}, u32[]{:S(2)}) async-start(f32[128,4,128]{2,1,0:T(4,128)} %bitcast.2), calls=%async_computation | async-start | bytes 524288 | tf_op jit(solution)/shard_map/all_to_all | solution.py:192
  25.7 0.7 copy-start.9
  46.1 0.7 copy-start.3
  46.1 0.7 copy-start.4
  75.7 0.7 copy-start.1
  75.7 0.7 copy-start.5
  75.7 0.7 copy-start.6
  107.3 28.8 %all-to-all-start.3 = ((f32[128,4,128]{2,1,0:T(4,128)}), f32[128,4,128]{2,1,0:T(4,128)S(1)}, u32[]{:S(2)}, u32[]{:S(2)}) async-start(f32[128,4,128]{2,1,0:T(4,128)} %bitcast.12), calls=%async_computation.3 | async-start | bytes 524288 | tf_op jit(solution)/shard_map/all_to_all | solution.py:192

commit v2 on v0

v2 whole, which is shorter than its diff:
```python
import functools

import jax
import jax.numpy as jnp
from jax import lax
from jax.experimental import pallas as pl
from jax.experimental.pallas import tpu as pltpu
from jax.sharding import PartitionSpec as P

STEP_TIME = 0.2
PLANE = 8
SINE = (25.132741928100586, -64.83582305908203, 67.0767593383789, -38.49842071533203, 14.06550407409668, -3.1933720111846924)
F32, BF16 = jnp.float32, jnp.bfloat16


def split(x):
    high = x.astype(BF16)
    return high, (x - high.astype(F32)).astype(BF16)


def both(x):
    return jnp.concatenate(split(x), axis=0)


def dot(a, b, axis):
    return lax.dot_general(a, b, (((1,), (axis,)), ((), ())), preferred_element_type=F32)


def product(halves, high, low, axis):
    traj = halves.shape[0] // 2
    first = dot(halves, high, axis)
    return first[:traj] + first[traj:] + dot(halves[:traj], low, axis)


def sine_of(residue, shift):
    turn = (residue << shift).astype(F32) * (2.0**-32)
    square = turn * turn
    value = jnp.full_like(square, SINE[-1])
    for factor in SINE[-2::-1]:
        value = value * square + factor
    return turn * (0.25 - square) * value


def advance_bonds(positions, velocities, pull, depth, stiffness, dipole_slope):
    damped = jnp.exp(-stiffness * positions)
    force = -2.0 * depth * stiffness * (1.0 - damped) * damped - dipole_slope * pull
    velocities = velocities + STEP_TIME * force
    return positions + STEP_TIME * velocities, velocities


def advance_modes(amplitudes, momenta, freq, coupling, drive):
    momenta = momenta + STEP_TIME * (-(freq * freq) * amplitudes - coupling * drive)
    return amplitudes + STEP_TIME * momenta, momenta


def start_kernel(positions, slope, sites, out_ref):
    dipole = slope[...] * positions[...]
    site = sites[...].astype(F32)
    rows = dipole.shape[0]
    for z in range(out_ref.shape[0] // (rows + 1)):
        out_ref[pl.ds(z * (rows + 1), rows), :] = dipole
        out_ref[pl.ds(z * (rows + 1) + rows, 1), :] = site


def first_kernel(shift, column, waves, amplitudes, momenta, freq, coupling, high_ref, low_ref, out_ref):
    traj, owned = amplitudes.shape
    mols = column.shape[1]
    depth = column.shape[0] // (traj + 1)
    modes = waves.shape[0]
    chunk = 4
    drive = None
    for start in range(0, depth, chunk):
        parts = []
        for z in range(start, start + chunk):
            at = z * (traj + 1)
            site = column[pl.ds(at + traj, 1), :].astype(jnp.int32)
            high, low = split(sine_of(waves[...] * site, shift))
            high_ref[:, pl.ds(z * mols, mols)] = high
            low_ref[:, pl.ds(z * mols, mols)] = low
            parts.append(both(column[pl.ds(at, traj), :]))
        columns = pl.ds(start * mols, chunk * mols)
        part = product(jnp.concatenate(parts, axis=1), high_ref[:, columns], low_ref[:, columns], 1)
        drive = part if drive is None else drive + part
    wide = lambda ref: jnp.broadcast_to(ref[...], (traj, owned))
    state = jnp.concatenate([amplitudes[...], momenta[...], wide(freq), wide(coupling)], axis=1)
    for peer in range(out_ref.shape[0]):
        out_ref[peer, :, :modes] = drive
        out_ref[peer, :, modes:] = state


def pull_blocks(weighted, high_ref, low_ref, out_ref):
    mols = out_ref.shape[2]
    pull = product(both(weighted), high_ref[...], low_ref[...], 0)
    for z in range(out_ref.shape[0]):
        out_ref[z] = pull[:, z * mols : (z + 1) * mols]


def modes_kernel(plane, high_ref, low_ref, amplitudes_out, momenta_out, freq_out, coupling_out, out_ref):
    peers = plane.shape[0]
    modes = amplitudes_out.shape[1]
    owned = modes // peers
    drive = plane[0, :, :modes]
    for peer in range(1, peers):
        drive = drive + plane[peer, :, :modes]
    whole = lambda i: jnp.concatenate(
        [plane[peer, :, modes + i * owned : modes + (i + 1) * owned] for peer in range(peers)], axis=1
    )
    freq, coupling = whole(2), whole(3)
    amplitudes, momenta = advance_modes(whole(0), whole(1), freq, coupling, drive)
    amplitudes_out[...] = amplitudes
    momenta_out[...] = momenta
    freq_out[...] = freq
    coupling_out[...] = coupling
    pull_blocks(coupling * amplitudes, high_ref, low_ref, out_ref)


def last_modes_kernel(plane, amplitudes, momenta, freq, coupling, high_ref, low_ref, amplitudes_out, momenta_out, out_ref):
    drive = plane[0]
    for peer in range(1, plane.shape[0]):
        drive = drive + plane[peer]
    new_amplitudes, new_momenta = advance_modes(amplitudes[...], momenta[...], freq[...], coupling[...], drive)
    amplitudes_out[...] = new_amplitudes
    momenta_out[...] = new_momenta
    pull_blocks(coupling[...] * new_amplitudes, high_ref, low_ref, out_ref)


def bonds_kernel(column, positions, velocities, depth, stiffness, slope, positions_out, velocities_out, *send):
    pull = column[0]
    for z in range(1, column.shape[0]):
        pull = pull + column[z]
    new_positions, new_velocities = advance_bonds(
        positions[...], velocities[...], pull, depth[...], stiffness[...], slope[...]
    )
    positions_out[...] = new_positions
    velocities_out[...] = new_velocities
    for out_ref in send:
        dipole = slope[...] * new_positions
        for z in range(out_ref.shape[0]):
            out_ref[z] = dipole


def drive_kernel(column, high_ref, low_ref, out_ref):
    dipole = jnp.concatenate([both(column[z]) for z in range(column.shape[0])], axis=1)
    drive = product(dipole, high_ref[...], low_ref[...], 1)
    for peer in range(out_ref.shape[0]):
        out_ref[peer] = drive


def call(kernel, outs, name, interpret=False):
    return pl.pallas_call(
        kernel,
        out_shape=[jax.ShapeDtypeStruct(shape, dtype) for shape, dtype in outs],
        name=name,
        interpret=interpret,
        compiler_params=None if interpret else pltpu.CompilerParams(vmem_limit_bytes=48 << 20),
    )


def stages(traj, mols, modes, owned, height, interpret=False):
    shift = 33 - (2 * mols * PLANE * height).bit_length()
    phase = ((modes, height * mols), BF16)
    bonds = ((traj, mols), F32)
    mode = ((traj, modes), F32)
    blocks = ((height, traj, mols), F32)
    made = dict(
        start=(start_kernel, [((height * (traj + 1), mols), F32)]),
        first=(functools.partial(first_kernel, shift), [phase, phase, ((PLANE, traj, modes + 4 * owned), F32)]),
        modes=(modes_kernel, [mode, mode, mode, mode, blocks]),
        bonds=(bonds_kernel, [bonds, bonds, blocks]),
        drive=(drive_kernel, [((PLANE, traj, modes), F32)]),
        last_modes=(last_modes_kernel, [mode, mode, blocks]),
        last_bonds=(bonds_kernel, [bonds, bonds]),
    )
    return {name: call(kernel, outs, name, interpret) for name, (kernel, outs) in made.items()}


def local(positions, velocities, amplitudes, momenta, sites, wavevectors, mode_freq, coupling, depth, stiffness, dipole_slope):
    height = lax.axis_size("mol") // PLANE
    traj, mols = positions.shape
    owned = amplitudes.shape[0]
    modes = PLANE * owned
    columns = [[z * PLANE + i for z in range(height)] for i in range(PLANE)]
    planes = [[z * PLANE + i for i in range(PLANE)] for z in range(height)]

    def exchange(blocks, groups):
        return lax.all_to_all(blocks, "mol", 0, 0, axis_index_groups=groups, tiled=True)

    call = stages(traj, mols, modes, owned, height)
    row = lambda x: x.reshape(1, -1)
    depth, stiffness, slope = row(depth), row(stiffness), row(dipole_slope)
    me = lax.axis_index("mol")
    waves = lax.dynamic_slice(wavevectors, (me // PLANE * modes,), (modes,)).reshape(modes, 1)

    (block,) = call["start"](positions, slope, row(sites))
    block = exchange(block.reshape(height, traj + 1, 1, mols), columns).reshape(-1, mols)
    high, low, block = call["first"](block, waves, amplitudes.T, momenta.T, row(mode_freq), row(coupling))
    *state, block = call["modes"](exchange(block, planes), high, low)
    positions, velocities, block = call["bonds"](exchange(block, columns), positions, velocities, depth, stiffness, slope)
    (block,) = call["drive"](exchange(block, columns), high, low)
    amplitudes, momenta, block = call["last_modes"](exchange(block, planes), *state, high, low)
    positions, velocities = call["last_bonds"](exchange(block, columns), positions, velocities, depth, stiffness, slope)
    mine = lambda x: lax.dynamic_slice(x, (0, me % PLANE * owned), (traj, owned)).T
    return positions, velocities, mine(amplitudes), mine(momenta)


def solution(mesh):
    bond, mode, mol = P("traj", "mol"), P("mol", "traj"), P("mol")
    return jax.shard_map(
        local,
        mesh=mesh,
        in_specs=(bond, bond, mode, mode, mol, P(), mol, mol, mol, mol, mol),
        out_specs=(bond, bond, mode, mode),
        check_vma=False,
    )
```

time: 797 us -> 113 us (0.14)
  the two profiles are of different devices: /device:TPU:1 before, /device:TPU:4 now
where the time goes in v2:
time: 113 us
  blocking collectives  55.6 us (49%)
  waiting for transfers between devices  28 us (25%)
  starting transfers between devices  18.7 us (17%)
  Pallas kernels  5.56 us (5%)
  local copies, waits for them, and re-layouts  4.27 us (4%)
    all_to_all x4, blocking collectives, exchange(): lax.all_to_all(blocks, 'mol', 0, 0, axis_index_groups=groups, tiled=True)  55.6 us
    all_to_all x2, waiting for transfers between devices, exchange(): lax.all_to_all(blocks, 'mol', 0, 0, axis_index_groups=groups, tiled=True)  28 us
    all_to_all x2, starting transfers between devices, exchange(): lax.all_to_all(blocks, 'mol', 0, 0, axis_index_groups=groups, tiled=True)  18.7 us
    unnamed x22, local copies, waits for them, and re-layouts  2.69 us
  transfers between devices with their start and end apart: 2, of which 2 were waited for; matrix products, arithmetic and copies ran while one was open for 1% of the time, Pallas kernels for 0%

profile of v2, /device:TPU:4, one launch (start us, length us, event | category | flops | bytes accessed | tf_op | source)
XLA Modules:
  0.0 112.9 jit_solution(16338944897429200235)
XLA Ops:
  0.6 0.0 copy-start.5
  0.6 0.0 copy-start.8
  0.7 0.6 copy-done.5
  1.3 0.0 copy-done.8
  1.3 0.0 copy-start
  1.3 0.7 copy-done
  2.0 0.7 start.1
  2.7 15.2 %all-to-all-start = ((f32[16,17,1,128]{3,2,1,0:T(1,128)}), f32[16,17,1,128]{3,2,1,0:T(1,128)S(1)}, u32[]{:S(2)}, u32[]{:S(2)}) async-start(f32[16,17,1,128]{3,2,1,0:T(1,128)} %bitcast.2), calls=%async_computation | async-start | bytes 278528 | tf_op jit(solution)/shard_map/all_to_all | solution.py:186
  17.9 0.8 dynamic_slice.9
  18.7 0.0 copy-start.3
  18.7 0.1 copy.17.waves
  18.8 0.0 copy-start.2
  18.8 14.0 %all-to-all-done = f32[16,17,1,128]{3,2,1,0:T(1,128)S(1)} async-done(((f32[16,17,1,128]{3,2,1,0:T(1,128)}), f32[16,17,1,128]{3,2,1,0:T(1,128)S(1)}, u32[]{:S(2)}, u32[]{:S(2)}) %all-to-all-start) | async-done | bytes 139296 | tf_op jit(solution)/shard_map/all_to_all | solution.py:186
  32.8 0.0 copy-start.9
  32.8 0.0 copy-start.10
  32.8 0.0 copy-done.3
  32.8 0.0 copy-done.2
  32.8 0.6 copy-done.9
  33.4 0.0 copy-done.10
  33.4 2.0 %first.1 = (bf16[256,2048]{1,0:T(8,128)(2,1)S(1)}, bf16[256,2048]{1,0:T(8,128)(2,1)S(1)}, f32[8,16,384]{2,1,0:T(8,128)S(1)}) custom-call(f32[272,128]{1,0:T(8,128)S(1)} %bitcast.15, s32[256,1]{1,0:T(8,128)S(1)} %copy.17.waves, f32[16,32]{1,0:T(8,128)S(1)} %bitcast.16, f32[16,32]{1,0:T(8,128)S(1)} %bitcast.17, f32[1,32]{1,0:T(1,128)S(1)} %bitcast.26, ...), custom_call_target="tpu_custom_call" | custom-call | tf_op jit(solution)/shard_map/first/pallas_call | solution.py:196
  35.4 11.1 %all_to_all.30.plane = f32[8,16,384]{2,1,0:T(8,128)S(1)} all-to-all(f32[8,16,384]{2,1,0:T(8,128)S(1)} %get-tuple-element.20), channel_id=1, replica_groups={{0,4,8,12,16,20,24,28},{32,36,40,44,48,52,56,60},{64,68,72,76,80,84,88,..., dimensions={0} | all-to-all | bytes 393216 | tf_op jit(solution)/shard_map/all_to_all | solution.py:186
  46.5 0.5 modes.1
  47.0 0.0 copy-start.1
  47.0 0.0 copy-start.4
  47.0 18.3 %all_to_all.31.column = f32[16,16,128]{2,1,0:T(8,128)S(1)} all-to-all(f32[16,16,128]{2,1,0:T(8,128)S(1)} %get-tuple-element.23), channel_id=1, replica_groups={{0,32,64,96,128,160,192,224,256,288,320,352,384,416,448,480},{4,36,68,1..., dimensions={0} | all-to-all | bytes 262144 | tf_op jit(solution)/shard_map/all_to_all | solution.py:186
  65.3 0.0 copy-start.6
  65.3 0.0 copy-start.7
  65.3 0.0 copy-done.1
  65.3 0.0 copy-done.4
  65.3 0.6 copy-done.6
  66.0 0.0 copy-done.7
  66.0 17.7 %all_to_all.32.column = f32[16,16,128]{2,1,0:T(8,128)S(1)} all-to-all(f32[16,16,128]{2,1,0:T(8,128)S(1)} %get-tuple-element.24), channel_id=1, replica_groups={{0,32,64,96,128,160,192,224,256,288,320,352,384,416,448,480},{4,36,68,1..., dimensions={0} | all-to-all | bytes 262144 | tf_op jit(solution)/shard_map/all_to_all | solution.py:186
  83.8 0.7 drive.1
  84.5 8.5 %all_to_all.33.plane = f32[8,16,256]{2,1,0:T(8,128)S(1)} all-to-all(f32[8,16,256]{2,1,0:T(8,128)S(1)} %drive.1), channel_id=1, replica_groups={{0,4,8,12,16,20,24,28},{32,36,40,44,48,52,56,60},{64,68,72,76,80,84,88,..., dimensions={0} | all-to-all | bytes 262144 | tf_op jit(solution)/shard_map/all_to_all | solution.py:186
  92.9 1.1 last_modes.1
  94.0 3.5 %all-to-all-start.5 = ((f32[16,16,128]{2,1,0:T(8,128)}), f32[16,16,128]{2,1,0:T(8,128)S(1)}, u32[]{:S(2)}, u32[]{:S(2)}) async-start(f32[16,16,128]{2,1,0:T(8,128)} %get-tuple-element.29), calls=%async_computation.5 | async-start | bytes 262144 | tf_op jit(solution)/shard_map/all_to_all | solution.py:186
  97.6 0.7 dynamic-slice_bitcast_fusion
  98.2 14.0 %all-to-all-done.5.column = f32[16,16,128]{2,1,0:T(8,128)S(1)} async-done(((f32[16,16,128]{2,1,0:T(8,128)}), f32[16,16,128]{2,1,0:T(8,128)S(1)}, u32[]{:S(2)}, u32[]{:S(2)}) %all-to-all-start.5) | async-done | bytes 131104 | tf_op jit(solution)/shard_map/all_to_all | solution.py:186
  112.3 0.6 last_bonds.1
  (1 shorter events, 0.0 us)
Async XLA Ops:
  0.6 0.7 copy-start.5
  0.6 0.7 copy-start.8
  1.3 0.7 copy-start
  2.7 30.1 %all-to-all-start = ((f32[16,17,1,128]{3,2,1,0:T(1,128)}), f32[16,17,1,128]{3,2,1,0:T(1,128)S(1)}, u32[]{:S(2)}, u32[]{:S(2)}) async-start(f32[16,17,1,128]{3,2,1,0:T(1,128)} %bitcast.2), calls=%async_computation | async-start | bytes 278528 | tf_op jit(solution)/shard_map/all_to_all | solution.py:186
  18.7 14.1 %copy-start.3 = (f32[32,16]{0,1:T(8,128)S(1)}, f32[32,16]{0,1:T(8,128)}, u32[]{:S(2)}) copy-start(f32[32,16]{0,1:T(8,128)} %param.14) | copy-start | bytes 6148
  18.8 14.0 %copy-start.2 = (f32[32,16]{0,1:T(8,128)S(1)}, f32[32,16]{0,1:T(8,128)}, u32[]{:S(2)}) copy-start(f32[32,16]{0,1:T(8,128)} %param.13) | copy-start | bytes 6148
  32.8 0.7 copy-start.9
  32.8 0.7 copy-start.10
  47.0 18.3 %copy-start.1 = (f32[16,128]{1,0:T(8,128)S(1)}, f32[16,128]{1,0:T(8,128)}, u32[]{:S(2)}) copy-start(f32[16,128]{1,0:T(8,128)} %positions.3) | copy-start | bytes 24580
  47.0 18.3 %copy-start.4 = (f32[16,128]{1,0:T(8,128)S(1)}, f32[16,128]{1,0:T(8,128)}, u32[]{:S(2)}) copy-start(f32[16,128]{1,0:T(8,128)} %velocities.1) | copy-start | bytes 24580
  65.3 0.7 copy-start.6
  65.3 0.7 copy-start.7
  94.0 18.2 %all-to-all-start.5 = ((f32[16,16,128]{2,1,0:T(8,128)}), f32[16,16,128]{2,1,0:T(8,128)S(1)}, u32[]{:S(2)}, u32[]{:S(2)}) async-start(f32[16,16,128]{2,1,0:T(8,128)} %get-tuple-element.29), calls=%async_computation.5 | async-start | bytes 262144 | tf_op jit(solution)/shard_map/all_to_all | solution.py:186

commit v3 on v2

v3 whole, which is shorter than its diff:
```python
import functools

import jax
import jax.numpy as jnp
from jax import lax
from jax.experimental import pallas as pl
from jax.experimental.pallas import tpu as pltpu
from jax.sharding import PartitionSpec as P

STEP_TIME = 0.2
PLANE = 8
LINE = 4
SINE = (25.132741928100586, -64.83582305908203, 67.0767593383789, -38.49842071533203, 14.06550407409668, -3.1933720111846924)
F32, BF16 = jnp.float32, jnp.bfloat16
SUB = 8
LANES = 128


def split(x):
    high = x.astype(BF16)
    return high, (x - high.astype(F32)).astype(BF16)


def both(x):
    return jnp.concatenate(split(x), axis=0)


def dot(a, b, axis):
    return lax.dot_general(a, b, (((1,), (axis,)), ((), ())), preferred_element_type=F32)


def product(halves, high, low, axis):
    traj = halves.shape[0] // 2
    first = dot(halves, high, axis)
    return first[:traj] + first[traj:] + dot(halves[:traj], low, axis)


def sine_of(residue, shift):
    turn = (residue << shift).astype(F32) * (2.0**-32)
    square = turn * turn
    value = jnp.full_like(square, SINE[-1])
    for factor in SINE[-2::-1]:
        value = value * square + factor
    return turn * (0.25 - square) * value


def morse(positions, depth, stiffness):
    damped = jnp.exp(-stiffness * positions)
    return -2.0 * depth * stiffness * (1.0 - damped) * damped


def advance_modes(amplitudes, momenta, freq, coupling, drive):
    momenta = momenta + STEP_TIME * (-(freq * freq) * amplitudes - coupling * drive)
    return amplitudes + STEP_TIME * momenta, momenta


def sum_over(ref, part=()):
    total = ref[(0, *part)]
    for i in range(1, ref.shape[0]):
        total = total + ref[(i, *part)]
    return total


def block_rows(traj):
    return 3 * traj + 3 - traj // 2


def start_kernel(positions, velocities, slope, sites, depth, stiffness, amplitudes, momenta, freq, coupling,
                 out_ref, free_positions, free_velocities, bond_ref, *scratch):
    hbm = (positions, velocities, slope, sites, depth, stiffness, amplitudes, momenta, freq, coupling)
    held, sems = scratch[:-1], scratch[-1]
    copies = [pltpu.make_async_copy(a, b, sems.at[i]) for i, (a, b) in enumerate(zip(hbm, held))]
    for copy in copies:
        copy.start()
    for copy in copies:
        copy.wait()
    positions, velocities, slope, sites, depth, stiffness, amplitudes, momenta, freq, coupling = (ref[...] for ref in held)
    traj, owned = amplitudes.shape
    half = traj // 2
    speed = velocities + STEP_TIME * morse(positions, depth, stiffness)
    moved = positions + STEP_TIME * speed
    free_positions[...] = moved
    free_velocities[...] = speed
    bond_ref[...] = jnp.concatenate([slope, depth, stiffness, jnp.zeros((SUB - 3, LANES), F32)], axis=0)
    modes = jnp.concatenate([amplitudes[:half], momenta[:half], amplitudes[half:], momenta[half:]], axis=1)
    own = jnp.concatenate([coupling, freq, coupling, freq], axis=1)
    rows = block_rows(traj)
    for z in range(out_ref.shape[0] // rows):
        at = z * rows
        for piece in (slope * positions, slope * moved, slope, sites.astype(F32), modes, own):
            out_ref[pl.ds(at, piece.shape[0]), :] = piece
            at += piece.shape[0]


def first_kernel(shift, traj, place, column, waves, high_ref, low_ref, free_ref, square_ref, out_ref, site_ref, dipole_ref):
    rows = block_rows(traj)
    half = traj // 2
    height = column.shape[0] // rows
    modes = waves.shape[0]
    chunk = modes // LINE
    for z in range(height):
        at = z * rows
        columns = pl.ds(z * LANES, LANES)
        dipole_ref[:, columns] = both(column[pl.ds(at, traj), :])
        free_ref[:, columns] = column[pl.ds(at + traj, traj), :]
        slope = column[pl.ds(at + 2 * traj, 1), :]
        square_ref[:, columns] = (STEP_TIME * STEP_TIME) * slope * slope
        site_ref[z] = column[pl.ds(at + 2 * traj + 1, 1), :].astype(jnp.int32)

    def fill(z, carry):
        columns = pl.ds(pl.multiple_of(z * LANES, LANES), LANES)
        site = site_ref[z]
        for part in range(LINE):
            taken = pl.ds(part * chunk, chunk)
            high, low = split(sine_of(waves[taken, :] * site, shift))
            high_ref[taken, columns] = high
            low_ref[taken, columns] = low
        return carry

    lax.fori_loop(0, height, fill, 0)
    drive = product(dipole_ref[...], high_ref[...], low_ref[...], 1)
    state = []
    own = []
    for quad in range(height // LINE):
        block = jnp.zeros((half + 1, LANES), F32)
        for i in range(LINE):
            at = (quad * LINE + i) * rows + 2 * traj + 2
            block = jnp.where(place[0] == i, column[pl.ds(at, half + 1), :], block)
        state.append(block[:half])
        own.append(block[half:])
    tail = jnp.concatenate(state + own + [jnp.zeros((SUB - len(own), LANES), F32)], axis=0)
    for peer in range(out_ref.shape[0]):
        for tile in range(modes // LANES):
            out_ref[peer, pl.ds(tile * traj, traj), :] = drive[:, tile * LANES : (tile + 1) * LANES]
        out_ref[peer, pl.ds(modes // LANES * traj, tail.shape[0]), :] = tail


def modes_kernel(owned, plane, high_ref, low_ref, amplitudes_out, momenta_out, freq_out, coupling_out, out_ref):
    traj, modes = amplitudes_out.shape
    half = traj // 2
    quads = modes // (PLANE * owned)
    base = modes // LANES * traj
    drive = jnp.concatenate(
        [sum_over(plane, (pl.ds(tile * traj, traj),)) for tile in range(modes // LANES)], axis=1
    )

    def gather(row, count, lane):
        return jnp.concatenate(
            [
                plane[peer, pl.ds(row(quad), count), lane * owned : (lane + 1) * owned]
                for quad in range(quads)
                for peer in range(PLANE)
            ],
            axis=1,
        )

    state = lambda quad: base + quad * half
    own = lambda quad: base + quads * half + quad
    amplitudes = jnp.concatenate([gather(state, half, 0), gather(state, half, 2)], axis=0)
    momenta = jnp.concatenate([gather(state, half, 1), gather(state, half, 3)], axis=0)
    coupling, freq = gather(own, 1, 0), gather(own, 1, 1)
    amplitudes, momenta = advance_modes(amplitudes, momenta, freq, coupling, drive)
    amplitudes_out[...] = amplitudes
    momenta_out[...] = momenta
    freq_out[...] = freq
    coupling_out[...] = coupling
    pull = product(both(coupling * amplitudes), high_ref[...], low_ref[...], 0)
    for peer in range(out_ref.shape[0]):
        for z in range(out_ref.shape[1] // traj):
            out_ref[peer, pl.ds(z * traj, traj), :] = pull[:, z * LANES : (z + 1) * LANES]


def middle_kernel(place, line, free_ref, square_ref, high_ref, low_ref, pull_out, out_ref):
    traj = pull_out.shape[0]
    own = jnp.zeros(pull_out.shape, F32)
    parts = []
    for z in range(line.shape[1] // traj):
        columns = pl.ds(z * LANES, LANES)
        pull = sum_over(line, (pl.ds(z * traj, traj),))
        own = jnp.where(place[1] == z, pull, own)
        parts.append(both(free_ref[:, columns] - square_ref[:, columns] * pull))
    pull_out[...] = own
    drive = product(jnp.concatenate(parts, axis=1), high_ref[...], low_ref[...], 1)
    for peer in range(out_ref.shape[0]):
        for tile in range(drive.shape[1] // LANES):
            out_ref[peer, pl.ds(tile * traj, traj), :] = drive[:, tile * LANES : (tile + 1) * LANES]


def last_modes_kernel(place, plane, amplitudes, momenta, freq, coupling, high_ref, low_ref, amplitudes_out, momenta_out, out_ref):
    traj, modes = amplitudes.shape
    drive = jnp.concatenate(
        [sum_over(plane, (pl.ds(tile * traj, traj),)) for tile in range(modes // LANES)], axis=1
    )
    new_amplitudes, new_momenta = advance_modes(amplitudes[...], momenta[...], freq[...], coupling[...], drive)
    amplitudes_out[...] = new_amplitudes
    momenta_out[...] = new_momenta
    width = LINE * LANES
    columns = pl.ds(pl.multiple_of(place[2] * width, width), width)
    pull = product(both(coupling[...] * new_amplitudes), high_ref[:, columns], low_ref[:, columns], 0)
    for i in range(LINE):
        out_ref[i] = pull[:, i * LANES : (i + 1) * LANES]


def last_kernel(line, pull, free_positions, free_velocities, bond_ref, positions_out, velocities_out):
    slope, depth, stiffness = (bond_ref[i : i + 1, :] for i in range(3))
    velocities = free_velocities[...] - STEP_TIME * (slope * pull[...])
    positions = free_positions[...] - STEP_TIME * (STEP_TIME * (slope * pull[...]))
    velocities = velocities + STEP_TIME * (morse(positions, depth, stiffness) - slope * sum_over(line))
    velocities_out[...] = velocities
    positions_out[...] = positions + STEP_TIME * velocities


def call(kernel, outs, name, scratch=(), places=False, inputs=None, interpret=False):
    def run(*args):
        vmem = pl.BlockSpec(memory_space=pltpu.VMEM)
        first = [pl.BlockSpec(memory_space=pltpu.SMEM)] if places else []
        specs = first + [vmem if inputs is None else pl.BlockSpec(memory_space=inputs)] * (len(args) - len(first))
        return pl.pallas_call(
            kernel,
            out_shape=[jax.ShapeDtypeStruct(shape, dtype) for shape, dtype in outs],
            in_specs=specs,
            out_specs=[vmem] * len(outs),
            scratch_shapes=list(scratch),
            name=name,
            interpret=interpret,
            compiler_params=None if interpret else pltpu.CompilerParams(vmem_limit_bytes=56 << 20),
        )(*args)

    return run


def stages(traj, mols, owned, height, interpret=False):
    modes = height // LINE * PLANE * owned
    lattice = 2 * mols * PLANE * height
    shift = 33 - lattice.bit_length()
    rows = block_rows(traj)
    here = height * mols
    tail = (height // LINE) * traj // 2 + SUB
    bond, row, mode, mode_row = (traj, mols), (1, mols), (traj, modes), (1, modes)
    own, own_row = (traj, owned), (1, owned)
    f = lambda *shape: (shape, F32)
    held = [pltpu.VMEM(s, F32) for s in (bond, bond, row)] + [pltpu.VMEM(row, jnp.int32)]
    held += [pltpu.VMEM(s, F32) for s in (row, row, own, own, own_row, own_row)]
    phase = ((modes, here), BF16)
    sent = modes // LANES * traj
    make = functools.partial(call, interpret=interpret)
    return dict(
        start=make(start_kernel, [f(height * rows, LANES), f(*bond), f(*bond), f(SUB, mols)], "start",
                   held + [pltpu.SemaphoreType.DMA((len(held),))], inputs=pl.ANY),
        first=make(functools.partial(first_kernel, shift, traj),
                   [phase, phase, f(traj, here), f(1, here), f(PLANE, sent + tail, LANES)], "first",
                   [pltpu.VMEM((height, 1, LANES), jnp.int32), pltpu.VMEM((2 * traj, here), BF16)], places=True),
        modes=make(functools.partial(modes_kernel, owned),
                   [f(*mode), f(*mode), f(*mode_row), f(*mode_row), f(LINE, height * traj, LANES)], "modes"),
        middle=make(middle_kernel, [f(*bond), f(PLANE, sent, LANES)], "middle", places=True),
        last_modes=make(last_modes_kernel, [f(*mode), f(*mode), f(LINE, traj, LANES)], "last_modes", places=True),
        last=make(last_kernel, [f(*bond), f(*bond)], "last"),
    )


def local(positions, velocities, amplitudes, momenta, sites, wavevectors, mode_freq, coupling, depth, stiffness, dipole_slope):
    height = lax.axis_size("mol") // PLANE
    traj, mols = positions.shape
    owned = amplitudes.shape[0]
    quads = height // LINE
    columns = [[z * PLANE + i for z in range(height)] for i in range(PLANE)]
    planes = [[z * PLANE + i for i in range(PLANE)] for z in range(height)]
    lines = [[(q * LINE + j) * PLANE + i for j in range(LINE)] for q in range(quads) for i in range(PLANE)]

    def exchange(blocks, groups):
        return lax.all_to_all(blocks, "mol", 0, 0, axis_index_groups=groups, tiled=True)

    run = stages(traj, mols, owned, height)
    row = lambda x: x.reshape(1, -1)
    me = lax.axis_index("mol")
    z, peer = me // PLANE, me % PLANE
    place = jnp.stack([z % LINE, z, z // LINE]).astype(jnp.int32)
    waves = lax.dynamic_slice(
        wavevectors.reshape(quads, -1), (0, z % LINE * PLANE * owned), (quads, PLANE * owned)
    ).reshape(-1, 1)

    block, free_positions, free_velocities, bond = run["start"](
        positions, velocities, row(dipole_slope), row(sites), row(depth), row(stiffness), amplitudes.T, momenta.T, row(mode_freq), row(coupling)
    )
    block = exchange(block.reshape(height, -1, 1, mols), columns).reshape(-1, mols)
    high, low, free, square, block = run["first"](place, block, waves)
    *state, block = run["modes"](exchange(block, planes), high, low)
    pull, block = run["middle"](place, exchange(block, lines), free, square, high, low)
    amplitudes, momenta, block = run["last_modes"](place, exchange(block, planes), *state, high, low)
    positions, velocities = run["last"](exchange(block, lines), pull, free_positions, free_velocities, bond)
    mine = lambda x: lax.dynamic_slice(x, (0, (z // LINE * PLANE + peer) * owned), (traj, owned)).T
    return positions, velocities, mine(amplitudes), mine(momenta)


def solution(mesh):
    bond, mode, mol = P("traj", "mol"), P("mol", "traj"), P("mol")
    return jax.shard_map(
        local,
        mesh=mesh,
        in_specs=(bond, bond, mode, mode, mol, P(), mol, mol, mol, mol, mol),
        out_specs=(bond, bond, mode, mode),
        check_vma=False,
    )
```

time: 113 us -> 132 us (1.17)
  the two profiles are of different devices: /device:TPU:4 before, /device:TPU:1 now
where the time goes in v3:
time: 132 us; the launch traced here: 130 us
  blocking collectives  40.7 us (31%)
  Pallas kernels  33 us (25%)
  waiting for transfers between devices  25.8 us (20%)
  starting transfers between devices  24.2 us (18%)
  local copies, waits for them, and re-layouts  5.35 us (4%)
    all_to_all x2, blocking collectives, exchange(): lax.all_to_all(blocks, 'mol', 0, 0, axis_index_groups=groups, tiled=True)  40.7 us
    pallas_call x6, Pallas kernels, run(): pl.pallas_call(kernel, out_shape=[jax.ShapeDtypeStruct(shape, dtype) for...  33 us
    all_to_all x3, waiting for transfers between devices, exchange(): lax.all_to_all(blocks, 'mol', 0, 0, axis_index_groups=groups, tiled=True)  25.8 us
    all_to_all x3, starting transfers between devices, exchange(): lax.all_to_all(blocks, 'mol', 0, 0, axis_index_groups=groups, tiled=True)  24.2 us
    unnamed x9, local copies, waits for them, and re-layouts  3.22 us
  transfers between devices with their start and end apart: 3, of which 3 were waited for; matrix products, arithmetic and copies ran while one was open for 3% of the time, Pallas kernels for 0%

profile of v3, /device:TPU:1, one launch (start us, length us, event | category | flops | bytes accessed | tf_op | source)
XLA Modules:
  0.0 130.4 jit_solution(7778033606080671692)
XLA Ops:
  0.6 1.7 %start.1 = (f32[688,128]{1,0:T(8,128)}, f32[16,128]{1,0:T(8,128)}, f32[16,128]{1,0:T(8,128)}, f32[8,128]{1,0:T(8,128)}) custom-call(f32[16,128]{1,0:T(8,128)} %positions.1, f32[16,128]{1,0:T(8,128)} %velocities.1, f32[1,128]{1,0:T(1,128)} %bitcast.28, s32[1,128]{1,0:T(1,128)} %bitcast.29, f32[1,128]{1,0:T(1,128)} %bitcast.30, f32[1,128]{1,0:T(1,128)} %bitcast.31, ...), custom_call_target="tpu_custom_call" | custom-call | tf_op jit(solution)/shard_map/start/pallas_call | solution.py:218
  2.4 15.7 %all-to-all-start = ((f32[16,43,1,128]{3,2,1,0:T(1,128)}), f32[16,43,1,128]{3,2,1,0:T(1,128)S(1)}, u32[]{:S(2)}, u32[]{:S(2)}) async-start(f32[16,43,1,128]{3,2,1,0:T(1,128)} %bitcast.24), calls=%async_computation | async-start | bytes 704512 | tf_op jit(solution)/shard_map/all_to_all | solution.py:271
  18.2 0.7 reshape.46
  18.9 1.0 copy.19
  19.9 0.6 pad_add_fusion.place
  20.5 13.4 %all-to-all-done = f32[16,43,1,128]{3,2,1,0:T(1,128)S(1)} async-done(((f32[16,43,1,128]{3,2,1,0:T(1,128)}), f32[16,43,1,128]{3,2,1,0:T(1,128)S(1)}, u32[]{:S(2)}, u32[]{:S(2)}) %all-to-all-start) | async-done | bytes 352288 | tf_op jit(solution)/shard_map/all_to_all | solution.py:271
  33.9 0.0 copy-start.1
  33.9 0.7 copy-done.1
  34.7 12.2 %first.1 = (bf16[1024,2048]{1,0:T(8,128)(2,1)}, bf16[1024,2048]{1,0:T(8,128)(2,1)}, f32[16,2048]{1,0:T(8,128)}, f32[1,2048]{1,0:T(1,128)}, f32[8,168,128]{2,1,0:T(8,128)}) custom-call(s32[3]{0:T(128)} %pad_add_fusion.place, f32[688,128]{1,0:T(8,128)} %bitcast.23, s32[1024,1]{1,0:T(8,128)} %bitcast.22), custom_call_target="tpu_custom_call" | custom-call | tf_op jit(solution)/shard_map/first/pallas_call | solution.py:218
  46.8 22.8 %all_to_all.25.plane = f32[8,168,128]{2,1,0:T(8,128)} all-to-all(f32[8,168,128]{2,1,0:T(8,128)} %get-tuple-element.26), channel_id=1, replica_groups={{0,4,8,12,16,20,24,28},{32,36,40,44,48,52,56,60},{64,68,72,76,80,84,88,..., dimensions={0} | all-to-all | bytes 1376256 | tf_op jit(solution)/shard_map/all_to_all | solution.py:271
  69.7 6.0 %modes.1 = (f32[16,1024]{1,0:T(8,128)}, f32[16,1024]{1,0:T(8,128)}, f32[1,1024]{1,0:T(1,128)}, f32[1,1024]{1,0:T(1,128)}, f32[4,256,128]{2,1,0:T(8,128)}) custom-call(f32[8,168,128]{2,1,0:T(8,128)} %all_to_all.25.plane, bf16[1024,2048]{1,0:T(8,128)(2,1)} %get-tuple-element.27.high_ref, bf16[1024,2048]{1,0:T(8,128)(2,1)} %get-tuple-element.28.low_ref), custom_call_target="tpu_custom_call" | custom-call | tf_op jit(solution)/shard_map/modes/pallas_call | solution.py:218
  75.6 17.8 %all_to_all.26.line = f32[4,256,128]{2,1,0:T(8,128)} all-to-all(f32[4,256,128]{2,1,0:T(8,128)} %get-tuple-element.29), channel_id=1, replica_groups={{0,32,64,96},{4,36,68,100},{8,40,72,104},{12,44,76,108},{16,48,80,112},..., dimensions={0} | all-to-all | bytes 1048576 | tf_op jit(solution)/shard_map/all_to_all | solution.py:271
  93.5 7.0 %middle.1 = (f32[16,128]{1,0:T(8,128)}, f32[8,128,128]{2,1,0:T(8,128)}) custom-call(s32[3]{0:T(128)} %pad_add_fusion.place, f32[4,256,128]{2,1,0:T(8,128)} %all_to_all.26.line, f32[16,2048]{1,0:T(8,128)} %get-tuple-element.30.free_ref, f32[1,2048]{1,0:T(1,128)} %get-tuple-element.31.square_ref, bf16[1024,2048]{1,0:T(8,128)(2,1)} %get-tuple-element.27.high_ref, ...), custom_call_target="tpu_custom_call" | custom-call | tf_op jit(solution)/shard_map/middle/pallas_call | solution.py:218
  100.4 5.2 %all-to-all-start.3 = ((f32[8,128,128]{2,1,0:T(8,128)}), f32[8,128,128]{2,1,0:T(8,128)S(1)}, u32[]{:S(2)}, u32[]{:S(2)}) async-start(f32[8,128,128]{2,1,0:T(8,128)} %get-tuple-element.32), calls=%async_computation.3 | async-start | bytes 1048576 | tf_op jit(solution)/shard_map/all_to_all | solution.py:271
  105.6 9.4 %all-to-all-done.3.plane = f32[8,128,128]{2,1,0:T(8,128)S(1)} async-done(((f32[8,128,128]{2,1,0:T(8,128)}), f32[8,128,128]{2,1,0:T(8,128)S(1)}, u32[]{:S(2)}, u32[]{:S(2)}) %all-to-all-start.3) | async-done | bytes 524320 | tf_op jit(solution)/shard_map/all_to_all | solution.py:271
  115.0 0.0 copy-start
  115.0 0.8 copy-done
  115.9 4.7 %last_modes.1 = (f32[16,1024]{1,0:T(8,128)}, f32[16,1024]{1,0:T(8,128)}, f32[4,16,128]{2,1,0:T(8,128)}) custom-call(s32[3]{0:T(128)} %pad_add_fusion.place, f32[8,128,128]{2,1,0:T(8,128)} %copy-done, f32[16,1024]{1,0:T(8,128)} %get-tuple-element.33.amplitudes, f32[16,1024]{1,0:T(8,128)} %get-tuple-element.34.momenta, f32[1,1024]{1,0:T(1,128)} %get-tuple-element.35.freq, ...), custom_call_target="tpu_custom_call" | custom-call | tf_op jit(solution)/shard_map/last_modes/pallas_call | solution.py:218
  120.6 3.3 %all-to-all-start.4 = ((f32[4,16,128]{2,1,0:T(8,128)}), f32[4,16,128]{2,1,0:T(8,128)S(1)}, u32[]{:S(2)}, u32[]{:S(2)}) async-start(f32[4,16,128]{2,1,0:T(8,128)} %get-tuple-element.37), calls=%async_computation.4 | async-start | bytes 65536 | tf_op jit(solution)/shard_map/all_to_all | solution.py:271
  123.9 1.4 %dynamic-slice_bitcast_fusion = (f32[32,16]{0,1:T(8,128)}, f32[32,16]{0,1:T(8,128)}) fusion(f32[16,1024]{1,0:T(8,128)} %get-tuple-element.45, s32[]{:T(128)S(6)} %select_n.34, f32[16,1024]{1,0:T(8,128)} %get-tuple-element.44), kind=kLoop, calls=%fused_computation | loop fusion | bytes 8196 | tf_op jit(solution)/shard_map/transpose | solution.py:291
  125.3 3.1 %all-to-all-done.4.line = f32[4,16,128]{2,1,0:T(8,128)S(1)} async-done(((f32[4,16,128]{2,1,0:T(8,128)}), f32[4,16,128]{2,1,0:T(8,128)S(1)}, u32[]{:S(2)}, u32[]{:S(2)}) %all-to-all-start.4) | async-done | bytes 32800 | tf_op jit(solution)/shard_map/all_to_all | solution.py:271
  128.4 0.0 copy-start.2
  128.4 0.6 copy-done.2
  129.0 1.4 %last.1 = (f32[16,128]{1,0:T(8,128)}, f32[16,128]{1,0:T(8,128)}) custom-call(f32[4,16,128]{2,1,0:T(8,128)} %copy-done.2, f32[16,128]{1,0:T(8,128)} %get-tuple-element.38.pull, f32[16,128]{1,0:T(8,128)} %get-tuple-element.39.free_positions, f32[16,128]{1,0:T(8,128)} %get-tuple-element.40.free_velocities, f32[8,128]{1,0:T(8,128)} %get-tuple-element.41.bond_ref), custom_call_target="tpu_custom_call" | custom-call | tf_op jit(solution)/shard_map/last/pallas_call | solution.py:218
  (2 shorter events, 0.0 us)
Async XLA Ops:
  2.4 31.6 %all-to-all-start = ((f32[16,43,1,128]{3,2,1,0:T(1,128)}), f32[16,43,1,128]{3,2,1,0:T(1,128)S(1)}, u32[]{:S(2)}, u32[]{:S(2)}) async-start(f32[16,43,1,128]{3,2,1,0:T(1,128)} %bitcast.24), calls=%async_computation | async-start | bytes 704512 | tf_op jit(solution)/shard_map/all_to_all | solution.py:271
  33.9 0.7 copy-start.1
  100.4 14.6 %all-to-all-start.3 = ((f32[8,128,128]{2,1,0:T(8,128)}), f32[8,128,128]{2,1,0:T(8,128)S(1)}, u32[]{:S(2)}, u32[]{:S(2)}) async-start(f32[8,128,128]{2,1,0:T(8,128)} %get-tuple-element.32), calls=%async_computation.3 | async-start | bytes 1048576 | tf_op jit(solution)/shard_map/all_to_all | solution.py:271
  115.0 0.8 copy-start
  120.6 7.7 %all-to-all-start.4 = ((f32[4,16,128]{2,1,0:T(8,128)}), f32[4,16,128]{2,1,0:T(8,128)S(1)}, u32[]{:S(2)}, u32[]{:S(2)}) async-start(f32[4,16,128]{2,1,0:T(8,128)} %get-tuple-element.37), calls=%async_computation.4 | async-start | bytes 65536 | tf_op jit(solution)/shard_map/all_to_all | solution.py:271
  128.4 0.6 copy-start.2

commit v4 on v3

v4 whole, which is shorter than its diff:
```python
import functools

import jax
import jax.numpy as jnp
from jax import lax
from jax.experimental import pallas as pl
from jax.experimental.pallas import tpu as pltpu
from jax.sharding import PartitionSpec as P

STEP_TIME = 0.2
SET = 16
SINE = (25.132741928100586, -64.83582305908203, 67.0767593383789, -38.49842071533203, 14.06550407409668, -3.1933720111846924)
F32, BF16 = jnp.float32, jnp.bfloat16
SUB = 8
LANES = 128


def split(x):
    high = x.astype(BF16)
    return high, (x - high.astype(F32)).astype(BF16)


def both(x):
    return jnp.concatenate(split(x), axis=0)


def dot(a, b, axis):
    return lax.dot_general(a, b, (((1,), (axis,)), ((), ())), preferred_element_type=F32)


def product(halves, high, low, axis):
    traj = halves.shape[0] // 2
    first = dot(halves, high, axis)
    return first[:traj] + first[traj:] + dot(halves[:traj], low, axis)


def sine_of(residue, shift):
    turn = (residue << shift).astype(F32) * (2.0**-32)
    square = turn * turn
    value = jnp.full_like(square, SINE[-1])
    for factor in SINE[-2::-1]:
        value = value * square + factor
    return turn * (0.25 - square) * value


def morse(positions, depth, stiffness):
    damped = jnp.exp(-stiffness * positions)
    return -2.0 * depth * stiffness * (1.0 - damped) * damped


def sum_over(ref, part=()):
    total = ref[(0, *part)]
    for i in range(1, ref.shape[0]):
        total = total + ref[(i, *part)]
    return total


def block_rows(traj):
    return 3 * traj + 3 - traj // 2


def start_kernel(positions, velocities, slope, sites, depth, stiffness, amplitudes, momenta, freq, coupling,
                 out_ref, free_positions, free_velocities, bond_ref, *scratch):
    hbm = (positions, velocities, slope, sites, depth, stiffness, amplitudes, momenta, freq, coupling)
    held, sems = scratch[:-1], scratch[-1]
    copies = [pltpu.make_async_copy(a, b, sems.at[i]) for i, (a, b) in enumerate(zip(hbm, held))]
    for copy in copies:
        copy.start()
    for copy in copies:
        copy.wait()
    positions, velocities, slope, sites, depth, stiffness, amplitudes, momenta, freq, coupling = (ref[...] for ref in held)
    traj, owned = amplitudes.shape
    half = traj // 2
    speed = velocities + STEP_TIME * morse(positions, depth, stiffness)
    moved = positions + STEP_TIME * speed
    free_positions[...] = moved
    free_velocities[...] = speed
    bond_ref[...] = jnp.concatenate([slope, depth, stiffness, jnp.zeros((SUB - 3, LANES), F32)], axis=0)
    modes = jnp.concatenate([amplitudes[:half], momenta[:half], amplitudes[half:], momenta[half:]], axis=1)
    own = jnp.concatenate([coupling, freq, coupling, freq], axis=1)
    rows = block_rows(traj)
    for block in range(out_ref.shape[0] // rows):
        at = block * rows
        for piece in (slope * positions, slope * moved, slope, sites.astype(F32), modes, own):
            out_ref[pl.ds(at, piece.shape[0]), :] = piece
            at += piece.shape[0]


def first_kernel(shift, traj, place, column, waves, high_ref, low_ref, free_ref, square_ref, amplitudes_ref, momenta_ref,
                 own_ref, place_out, out_ref, dipole_ref):
    place_out[0] = place[0]
    rows = block_rows(traj)
    half = traj // 2
    sets = column.shape[0] // rows
    chunk = out_ref.shape[2]
    owned = chunk // sets
    sites = []
    for q in range(sets):
        at = q * rows
        columns = pl.ds(q * LANES, LANES)
        dipole_ref[:, columns] = both(column[pl.ds(at, traj), :])
        free_ref[:, columns] = column[pl.ds(at + traj, traj), :]
        slope = column[pl.ds(at + 2 * traj, 1), :]
        square_ref[:, columns] = (STEP_TIME * STEP_TIME) * slope * slope
        sites.append(column[pl.ds(at + 2 * traj + 1, 1), :].astype(jnp.int32))

    def gather(row, count, lane):
        return jnp.concatenate(
            [column[pl.ds(q * rows + row, count), lane * owned : (lane + 1) * owned] for q in range(sets)], axis=1
        )

    at = 2 * traj + 2
    amplitudes_ref[...] = jnp.concatenate([gather(at, half, 0), gather(at, half, 2)], axis=0)
    momenta_ref[...] = jnp.concatenate([gather(at, half, 1), gather(at, half, 3)], axis=0)
    own_ref[...] = jnp.concatenate([gather(at + half, 1, 0), gather(at + half, 1, 1)], axis=0)

    def fill(member, carry):
        taken = pl.ds(pl.multiple_of(member * chunk, chunk), chunk)
        wave = waves[taken, :]
        drive = None
        parts = 2
        for part in range(parts):
            for q in range(part * sets // parts, (part + 1) * sets // parts):
                columns = pl.ds(q * LANES, LANES)
                high, low = split(sine_of(wave * sites[q], shift))
                high_ref[taken, columns] = high
                low_ref[taken, columns] = low
            columns = pl.ds(part * sets // parts * LANES, sets // parts * LANES)
            piece = product(dipole_ref[:, columns], high_ref[taken, columns], low_ref[taken, columns], 1)
            drive = piece if drive is None else drive + piece
        out_ref[member] = drive
        return carry

    lax.fori_loop(0, out_ref.shape[0], fill, 0)


def modes_kernel(received, amplitudes, momenta, own, amplitudes_out, momenta_out, out_ref):
    drive = sum_over(received)
    coupling, freq = own[0:1, :], own[1:2, :]
    new_momenta = momenta[...] + STEP_TIME * (-(freq * freq) * amplitudes[...] - coupling * drive)
    new_amplitudes = amplitudes[...] + STEP_TIME * new_momenta
    momenta_out[...] = new_momenta
    amplitudes_out[...] = new_amplitudes
    weighted = coupling * new_amplitudes
    for member in range(out_ref.shape[0]):
        out_ref[member] = weighted


def pull_of(received, high_ref, low_ref, columns):
    chunk = received.shape[2]
    pull = None
    for member in range(received.shape[0]):
        rows = pl.ds(member * chunk, chunk)
        piece = product(both(received[member]), high_ref[rows, columns], low_ref[rows, columns], 0)
        pull = piece if pull is None else pull + piece
    return pull


def middle_kernel(place, received, free_ref, square_ref, high_ref, low_ref, pull_out, out_ref):
    pull = pull_of(received, high_ref, low_ref, slice(None))
    own = pull[:, :LANES]
    for q in range(1, pull.shape[1] // LANES):
        own = jnp.where(place[0] == q, pull[:, q * LANES : (q + 1) * LANES], own)
    pull_out[...] = own
    dipole = both(free_ref[...] - square_ref[...] * pull)
    chunk = out_ref.shape[2]
    for member in range(out_ref.shape[0]):
        rows = pl.ds(member * chunk, chunk)
        out_ref[member] = product(dipole, high_ref[rows, :], low_ref[rows, :], 1)


def last_kernel(place, received, high_ref, low_ref, pull, free_positions, free_velocities, bond_ref, amplitudes, momenta,
                positions_out, velocities_out, amplitudes_out, momenta_out):
    owned = amplitudes_out.shape[1]
    for whole, own in ((amplitudes, amplitudes_out), (momenta, momenta_out)):
        mine = whole[:, :owned]
        for q in range(1, whole.shape[1] // owned):
            mine = jnp.where(place[0] == q, whole[:, q * owned : (q + 1) * owned], mine)
        own[...] = mine
    columns = pl.ds(pl.multiple_of(place[0] * LANES, LANES), LANES)
    last_pull = pull_of(received, high_ref, low_ref, columns)
    slope, depth, stiffness = (bond_ref[i : i + 1, :] for i in range(3))
    first = slope * pull[...]
    velocities = free_velocities[...] - STEP_TIME * first
    positions = free_positions[...] - STEP_TIME * (STEP_TIME * first)
    velocities = velocities + STEP_TIME * (morse(positions, depth, stiffness) - slope * last_pull)
    velocities_out[...] = velocities
    positions_out[...] = positions + STEP_TIME * velocities


def call(kernel, outs, name, spaces, scratch=(), grant=20, interpret=False):
    kinds = {"V": pltpu.VMEM, "S": pltpu.SMEM, "H": pltpu.HBM}
    return pl.pallas_call(
        kernel,
        out_shape=[jax.ShapeDtypeStruct(shape, dtype) for shape, dtype in outs],
        in_specs=[pl.BlockSpec(memory_space=kinds[letter]) for letter in spaces],
        out_specs=[pl.BlockSpec(memory_space=kinds["S" if dtype == jnp.int32 else "V"]) for _, dtype in outs],
        scratch_shapes=list(scratch),
        name=name,
        interpret=interpret,
        compiler_params=None if interpret else pltpu.CompilerParams(vmem_limit_bytes=grant << 20),
    )


def stages(traj, mols, owned, sets, interpret=False):
    lattice = 2 * mols * SET * sets
    shift = 33 - lattice.bit_length()
    modes, chunk, here = sets * SET * owned, sets * owned, sets * mols
    bond, row, own, own_row = (traj, mols), (1, mols), (traj, owned), (1, owned)
    f = lambda *shape: (shape, F32)
    held = [pltpu.VMEM(s, F32) for s in (bond, bond, row)] + [pltpu.VMEM(row, jnp.int32)]
    held += [pltpu.VMEM(s, F32) for s in (row, row, own, own, own_row, own_row)]
    phase = ((modes, here), BF16)
    state, blocks = f(traj, chunk), f(SET, traj, chunk)
    make = functools.partial(call, interpret=interpret)
    return dict(
        start=make(start_kernel, [f(sets * block_rows(traj), LANES), f(*bond), f(*bond), f(SUB, mols)], "start", 10 * "H",
                   held + [pltpu.SemaphoreType.DMA((len(held),))], grant=56),
        first=make(functools.partial(first_kernel, shift, traj),
                   [phase, phase, f(traj, here), f(1, here), state, state, f(2, chunk), ((1,), jnp.int32), blocks], "first", "SVV",
                   [pltpu.VMEM((2 * traj, here), BF16)]),
        modes=make(modes_kernel, [state, state, blocks], "modes", "VVVV"),
        middle=make(middle_kernel, [f(*bond), blocks], "middle", "SVVVVV"),
        last=make(last_kernel, [f(*bond), f(*bond), f(*own), f(*own)], "last", "S" + 9 * "V"),
    )


def local(positions, velocities, amplitudes, momenta, sites, wavevectors, mode_freq, coupling, depth, stiffness, dipole_slope):
    sets = lax.axis_size("mol") // SET
    traj, mols = positions.shape
    owned = amplitudes.shape[0]
    across = [[q * SET + i for q in range(sets)] for i in range(SET)]
    inside = [[q * SET + i for i in range(SET)] for q in range(sets)]

    def exchange(blocks, groups):
        return lax.all_to_all(blocks, "mol", 0, 0, axis_index_groups=groups, tiled=True)

    run = stages(traj, mols, owned, sets)
    row = lambda x: x.reshape(1, -1)
    place = (lax.axis_index("mol") // SET).astype(jnp.int32).reshape(1)
    waves = wavevectors.reshape(sets, SET, owned).transpose(1, 0, 2).reshape(-1, 1)

    block, free_positions, free_velocities, bond = run["start"](
        positions, velocities, row(dipole_slope), row(sites), row(depth), row(stiffness), amplitudes.T, momenta.T, row(mode_freq), row(coupling)
    )
    block = exchange(block.reshape(sets, -1, 1, mols), across).reshape(-1, mols)
    high, low, free, square, amplitudes, momenta, own, place, block = run["first"](place, block, waves)
    amplitudes, momenta, block = run["modes"](exchange(block, inside), amplitudes, momenta, own)
    pull, block = run["middle"](place, exchange(block, inside), free, square, high, low)
    amplitudes, momenta, block = run["modes"](exchange(block, inside), amplitudes, momenta, own)
    positions, velocities, amplitudes, momenta = run["last"](
        place, exchange(block, inside), high, low, pull, free_positions, free_velocities, bond, amplitudes, momenta
    )
    return positions, velocities, amplitudes.T, momenta.T


def solution(mesh):
    bond, mode, mol = P("traj", "mol"), P("mol", "traj"), P("mol")
    return jax.shard_map(
        local,
        mesh=mesh,
        in_specs=(bond, bond, mode, mode, mol, P(), mol, mol, mol, mol, mol),
        out_specs=(bond, bond, mode, mode),
        check_vma=False,
    )
```

time: 132 us -> 110 us (0.83)
  waiting for transfers between devices: 25.8 us -> 11.8 us
  starting transfers between devices: 24.2 us -> 15.6 us
  blocking collectives: 40.7 us -> 47.3 us
  local copies, waits for them, and re-layouts: 5.35 us -> 2.98 us
  Pallas kernels: 33 us -> 31.1 us
    all_to_all x3 -> x1, waiting for transfers between devices: 25.8 us -> 11.8 us  [exchange(): lax.all_to_all(blocks, 'mol', 0, 0, axis_index_groups=groups, tiled=True)]
    all_to_all x3 -> x1, starting transfers between devices: 24.2 us -> 15.6 us  [exchange(): lax.all_to_all(blocks, 'mol', 0, 0, axis_index_groups=groups, tiled=True)]
    all_to_all x2 -> x4, blocking collectives: 40.7 us -> 47.3 us  [exchange(): lax.all_to_all(blocks, 'mol', 0, 0, axis_index_groups=groups, tiled=True)]
    unnamed x9 -> x6, local copies, waits for them, and re-layouts: 3.22 us -> 0.01 us
    reshape x1 -> x2, local copies, waits for them, and re-layouts: 0.73 us -> 2.94 us  [local(): wavevectors.reshape(sets, SET, owned).transpose(1, 0, 2).reshape(-1, 1)]
    pallas_call x6, Pallas kernels: 33 us -> 31.1 us  [the longest x1 19.6 us: local(): run['first'](place, block, waves)]
    transpose x1, local copies, waits for them, and re-layouts: 1.4 us -> 0.03 us  [local(): wavevectors.reshape(sets, SET, owned).transpose(1, 0, 2).reshape(-1, 1)]
  transfers between devices with their start and end apart: 3 -> 1, of which waited for: 3 -> 1; matrix products, arithmetic and copies ran while one was open for 3% -> 3% of each run, Pallas kernels for 0% -> 0%
where the time goes in v4:
time: 110 us
  blocking collectives  47.3 us (43%)
  Pallas kernels  31.1 us (28%)
  starting transfers between devices  15.6 us (14%)
  waiting for transfers between devices  11.8 us (11%)
  local copies, waits for them, and re-layouts  2.98 us (3%)
    all_to_all x4, blocking collectives, exchange(): lax.all_to_all(blocks, 'mol', 0, 0, axis_index_groups=groups, tiled=True)  47.3 us
    pallas_call x1, Pallas kernels, local(): run['first'](place, block, waves)  19.6 us
    all_to_all x1, starting transfers between devices, exchange(): lax.all_to_all(blocks, 'mol', 0, 0, axis_index_groups=groups, tiled=True)  15.6 us
    all_to_all x1, waiting for transfers between devices, exchange(): lax.all_to_all(blocks, 'mol', 0, 0, axis_index_groups=groups, tiled=True)  11.8 us
    pallas_call x1, Pallas kernels, local(): run['middle'](place, exchange(block, inside), free, square, high, low)  7.72 us
    reshape x2, local copies, waits for them, and re-layouts, local(): wavevectors.reshape(sets, SET, owned).transpose(1, 0, 2).reshape(-1, 1)  2.94 us
  transfers between devices with their start and end apart: 1, of which 1 were waited for; matrix products, arithmetic and copies ran while one was open for 3% of the time, Pallas kernels for 0%

profile of v4, /device:TPU:1, one launch (start us, length us, event | category | flops | bytes accessed | tf_op | source)
XLA Modules:
  0.0 109.5 jit_solution(15258813859676538485)
XLA Ops:
  0.6 1.7 %start.1 = (f32[344,128]{1,0:T(8,128)}, f32[16,128]{1,0:T(8,128)}, f32[16,128]{1,0:T(8,128)}, f32[8,128]{1,0:T(8,128)}) custom-call(f32[16,128]{1,0:T(8,128)} %positions.1, f32[16,128]{1,0:T(8,128)} %velocities.1, f32[1,128]{1,0:T(1,128)} %bitcast.19, s32[1,128]{1,0:T(1,128)} %bitcast.20, f32[1,128]{1,0:T(1,128)} %bitcast.21, f32[1,128]{1,0:T(1,128)} %bitcast.22, ...), custom_call_target="tpu_custom_call" | custom-call | tf_op jit(solution)/shard_map/start/pallas_call | solution.py:243
  2.3 15.6 %all-to-all-start = ((f32[8,43,1,128]{3,2,1,0:T(1,128)}), f32[8,43,1,128]{3,2,1,0:T(1,128)S(1)}, u32[]{:S(2)}, u32[]{:S(2)}) async-start(f32[8,43,1,128]{3,2,1,0:T(1,128)} %bitcast.16), calls=%async_computation | async-start | bytes 352256 | tf_op jit(solution)/shard_map/all_to_all | solution.py:236
  17.9 0.8 reshape.50
  18.8 2.1 %reshape.52.waves = s32[4096,1]{1,0:T(8,128)S(1)} reshape(s32[16,8,32]{2,1,0:T(8,128)S(1)} %copy.18) | data formatting | bytes 32768 | tf_op jit(solution)/shard_map/reshape | solution.py:241
  20.9 11.8 %all-to-all-done = f32[8,43,1,128]{3,2,1,0:T(1,128)S(1)} async-done(((f32[8,43,1,128]{3,2,1,0:T(1,128)}), f32[8,43,1,128]{3,2,1,0:T(1,128)S(1)}, u32[]{:S(2)}, u32[]{:S(2)}) %all-to-all-start) | async-done | bytes 176160 | tf_op jit(solution)/shard_map/all_to_all | solution.py:236
  32.7 19.6 %first.1 = (bf16[4096,1024]{1,0:T(8,128)(2,1)S(1)}, bf16[4096,1024]{1,0:T(8,128)(2,1)S(1)}, f32[16,1024]{1,0:T(8,128)S(1)}, f32[1,1024]{1,0:T(1,128)S(1)}, f32[1...) custom-call(s32[1]{0:T(128)} %bitcast.place, ...), custom_call_target="tpu_custom_call" | custom-call | tf_op jit(solution)/shard_map/first/pallas_call | solution.py:247
  52.3 15.4 %all_to_all.25.received = f32[16,16,256]{2,1,0:T(8,128)S(1)} all-to-all(f32[16,16,256]{2,1,0:T(8,128)S(1)} %get-tuple-element.31), channel_id=1, replica_groups={{0,4,8,12,16,20,24,28,32,36,40,44,48,52,56,60},{64,68,72,76,80,84,88,92..., dimensions={0} | all-to-all | bytes 524288 | tf_op jit(solution)/shard_map/all_to_all | solution.py:236
  67.8 10.6 %all_to_all.26.received = f32[16,16,256]{2,1,0:T(8,128)S(1)} all-to-all(f32[16,16,256]{2,1,0:T(8,128)S(1)} %get-tuple-element.35), channel_id=1, replica_groups={{0,4,8,12,16,20,24,28,32,36,40,44,48,52,56,60},{64,68,72,76,80,84,88,92..., dimensions={0} | all-to-all | bytes 524288 | tf_op jit(solution)/shard_map/all_to_all | solution.py:236
  78.4 0.0 copy-start
  78.4 0.0 copy-start.1
  78.4 0.0 copy-start.2
  78.4 7.7 %middle.1 = (f32[16,128]{1,0:T(8,128)S(1)}, f32[16,16,256]{2,1,0:T(8,128)S(1)}) custom-call(s32[1]{0:T(128)} %get-tuple-element.30.place, f32[16,16,256]{2,1,0:T(8,128)S(1)} %all_to_all.26.received, f32[16,1024]{1,0:T(8,128)S(1)} %get-tuple-element.36.free_ref, f32[1,1024]{1,0:T(1,128)S(1)} %get-tuple-element.37.square_ref, ...), custom_call_target="tpu_custom_call" | custom-call | tf_op jit(solution)/shard_map/middle/pallas_call | solution.py:249
  86.2 10.6 %all_to_all.27.received = f32[16,16,256]{2,1,0:T(8,128)S(1)} all-to-all(f32[16,16,256]{2,1,0:T(8,128)S(1)} %get-tuple-element.40), channel_id=1, replica_groups={{0,4,8,12,16,20,24,28,32,36,40,44,48,52,56,60},{64,68,72,76,80,84,88,92..., dimensions={0} | all-to-all | bytes 524288 | tf_op jit(solution)/shard_map/all_to_all | solution.py:236
  96.8 10.6 %all_to_all.28.received = f32[16,16,256]{2,1,0:T(8,128)S(1)} all-to-all(f32[16,16,256]{2,1,0:T(8,128)S(1)} %get-tuple-element.43), channel_id=1, replica_groups={{0,4,8,12,16,20,24,28,32,36,40,44,48,52,56,60},{64,68,72,76,80,84,88,92..., dimensions={0} | all-to-all | bytes 524288 | tf_op jit(solution)/shard_map/all_to_all | solution.py:236
  107.5 0.0 copy-done
  107.5 0.0 copy-done.1
  107.5 0.0 copy-done.2
  107.5 2.1 %last.1 = (f32[16,128]{1,0:T(8,128)}, f32[16,128]{1,0:T(8,128)}, f32[16,32]{1,0:T(8,128)}, f32[16,32]{1,0:T(8,128)}) custom-call(s32[1]{0:T(128)} %get-tuple-element.30.place, f32[16,16,256]{2,1,0:T(8,128)S(1)} %all_to_all.28.received, bf16[4096,1024]{1,0:T(8,128)(2,1)S(1)} %get-tuple-element.38.high_ref, bf16[4096,1024]{1,0:T(8,128)(2,1)S(1)} %get-tuple-element.39.low_ref, ...), custom_call_target="tpu_custom_call" | custom-call | tf_op jit(solution)/shard_map/last/pallas_call | solution.py:251
  (3 shorter events, 0.1 us)
Async XLA Ops:
  2.3 30.5 %all-to-all-start = ((f32[8,43,1,128]{3,2,1,0:T(1,128)}), f32[8,43,1,128]{3,2,1,0:T(1,128)S(1)}, u32[]{:S(2)}, u32[]{:S(2)}) async-start(f32[8,43,1,128]{3,2,1,0:T(1,128)} %bitcast.16), calls=%async_computation | async-start | bytes 352256 | tf_op jit(solution)/shard_map/all_to_all | solution.py:236
  78.4 29.0 %copy-start = (f32[16,128]{1,0:T(8,128)S(1)}, f32[16,128]{1,0:T(8,128)}, u32[]{:S(2)}) copy-start(f32[16,128]{1,0:T(8,128)} %get-tuple-element.45.free_positions) | copy-start | bytes 24580
  78.4 29.0 %copy-start.1 = (f32[16,128]{1,0:T(8,128)S(1)}, f32[16,128]{1,0:T(8,128)}, u32[]{:S(2)}) copy-start(f32[16,128]{1,0:T(8,128)} %get-tuple-element.46.free_velocities) | copy-start | bytes 24580
  78.4 29.0 %copy-start.2 = (f32[8,128]{1,0:T(8,128)S(1)}, f32[8,128]{1,0:T(8,128)}, u32[]{:S(2)}) copy-start(f32[8,128]{1,0:T(8,128)} %get-tuple-element.47.bond_ref) | copy-start | bytes 12292

commit v5 on v4

--- a/solution.py
+++ b/solution.py
@@ -9,7 +9,7 @@
 
 STEP_TIME = 0.2
 SET = 16
-SINE = (25.132741928100586, -64.83582305908203, 67.0767593383789, -38.49842071533203, 14.06550407409668, -3.1933720111846924)
+SINE = (25.13273048400879, -64.83467864990234, 67.04389953613281, -38.12319564819336, 12.233302116394043)
 F32, BF16 = jnp.float32, jnp.bfloat16
 SUB = 8
 LANES = 128
@@ -34,11 +34,11 @@
     return first[:traj] + first[traj:] + dot(halves[:traj], low, axis)
 
 
-def sine_of(residue, shift):
-    turn = (residue << shift).astype(F32) * (2.0**-32)
+def sine_of(product):
+    turn = product.astype(F32) * (2.0**-32)
     square = turn * turn
-    value = jnp.full_like(square, SINE[-1])
-    for factor in SINE[-2::-1]:
+    value = square * SINE[-1] + SINE[-2]
+    for factor in SINE[-3::-1]:
         value = value * square + factor
     return turn * (0.25 - square) * value
 
@@ -87,7 +87,7 @@
 
 
 def first_kernel(shift, traj, place, column, waves, high_ref, low_ref, free_ref, square_ref, amplitudes_ref, momenta_ref,
-                 own_ref, place_out, out_ref, dipole_ref):
+                 own_ref, place_out, out_ref, dipole_ref, held_high, held_low):
     place_out[0] = place[0]
     rows = block_rows(traj)
     half = traj // 2
@@ -102,7 +102,7 @@
         free_ref[:, columns] = column[pl.ds(at + traj, traj), :]
         slope = column[pl.ds(at + 2 * traj, 1), :]
         square_ref[:, columns] = (STEP_TIME * STEP_TIME) * slope * slope
-        sites.append(column[pl.ds(at + 2 * traj + 1, 1), :].astype(jnp.int32))
+        sites.append(column[pl.ds(at + 2 * traj + 1, 1), :].astype(jnp.int32) << shift)
 
     def gather(row, count, lane):
         return jnp.concatenate(
@@ -114,24 +114,32 @@
     momenta_ref[...] = jnp.concatenate([gather(at, half, 1), gather(at, half, 3)], axis=0)
     own_ref[...] = jnp.concatenate([gather(at + half, 1, 0), gather(at + half, 1, 1)], axis=0)
 
-    def fill(member, carry):
+    def fill(member, slot):
         taken = pl.ds(pl.multiple_of(member * chunk, chunk), chunk)
         wave = waves[taken, :]
-        drive = None
-        parts = 2
-        for part in range(parts):
-            for q in range(part * sets // parts, (part + 1) * sets // parts):
-                columns = pl.ds(q * LANES, LANES)
-                high, low = split(sine_of(wave * sites[q], shift))
-                high_ref[taken, columns] = high
-                low_ref[taken, columns] = low
-            columns = pl.ds(part * sets // parts * LANES, sets // parts * LANES)
-            piece = product(dipole_ref[:, columns], high_ref[taken, columns], low_ref[taken, columns], 1)
-            drive = piece if drive is None else drive + piece
-        out_ref[member] = drive
+        for q in range(sets):
+            columns = pl.ds(q * LANES, LANES)
+            high, low = split(sine_of(wave * sites[q]))
+            high_ref[taken, columns] = high
+            low_ref[taken, columns] = low
+            held_high[slot, :, columns] = high
+            held_low[slot, :, columns] = low
+
+    def finish(member, slot):
+        out_ref[member] = product(dipole_ref[...], held_high[slot], held_low[slot], 1)
+
+    def step(pair, carry):
+        for slot in range(2):
+            finish(2 * pair + slot, slot)
+            fill(2 * pair + slot + 1, 1 - slot)
         return carry
 
-    lax.fori_loop(0, out_ref.shape[0], fill, 0)
+    members = out_ref.shape[0]
+    fill(0, 0)
+    lax.fori_loop(0, members // 2 - 1, step, 0)
+    finish(members - 2, 0)
+    fill(members - 1, 1)
+    finish(members - 1, 1)
 
 
 def modes_kernel(received, amplitudes, momenta, own, amplitudes_out, momenta_out, out_ref):
@@ -218,7 +226,7 @@
                    held + [pltpu.SemaphoreType.DMA((len(held),))], grant=56),
         first=make(functools.partial(first_kernel, shift, traj),
                    [phase, phase, f(traj, here), f(1, here), state, state, f(2, chunk), ((1,), jnp.int32), blocks], "first", "SVV",
-                   [pltpu.VMEM((2 * traj, here), BF16)]),
+                   [pltpu.VMEM((2 * traj, here), BF16)] + 2 * [pltpu.VMEM((2, chunk, here), BF16)]),
         modes=make(modes_kernel, [state, state, blocks], "modes", "VVVV"),
         middle=make(middle_kernel, [f(*bond), blocks], "middle", "SVVVVV"),
         last=make(last_kernel, [f(*bond), f(*bond), f(*own), f(*own)], "last", "S" + 9 * "V"),

time: 110 us -> 105 us (0.955)
  Pallas kernels: 31.1 us -> 26.2 us
    pallas_call x1, Pallas kernels: 19.6 us -> 14.7 us  [local(): run['first'](place, block, waves)]
where the time goes in v5:
time: 105 us
  blocking collectives  47.3 us (45%)
  Pallas kernels  26.2 us (25%)
  starting transfers between devices  15.6 us (15%)
  waiting for transfers between devices  11.8 us (11%)
  local copies, waits for them, and re-layouts  2.98 us (3%)
    all_to_all x4, blocking collectives, exchange(): lax.all_to_all(blocks, 'mol', 0, 0, axis_index_groups=groups, tiled=True)  47.3 us
    all_to_all x1, starting transfers between devices, exchange(): lax.all_to_all(blocks, 'mol', 0, 0, axis_index_groups=groups, tiled=True)  15.6 us
    pallas_call x1, Pallas kernels, local(): run['first'](place, block, waves)  14.7 us
    all_to_all x1, waiting for transfers between devices, exchange(): lax.all_to_all(blocks, 'mol', 0, 0, axis_index_groups=groups, tiled=True)  11.8 us
    pallas_call x1, Pallas kernels, local(): run['middle'](place, exchange(block, inside), free, square, high, low)  7.72 us
    reshape x2, local copies, waits for them, and re-layouts, local(): wavevectors.reshape(sets, SET, owned).transpose(1, 0, 2).reshape(-1, 1)  2.94 us
  transfers between devices with their start and end apart: 1, of which 1 were waited for; matrix products, arithmetic and copies ran while one was open for 3% of the time, Pallas kernels for 0%

profile of v5, /device:TPU:1, one launch (start us, length us, event | category | flops | bytes accessed | tf_op | source)
XLA Modules:
  0.0 104.6 jit_solution(5599569686155958494)
XLA Ops:
  0.6 1.7 %start.1 = (f32[344,128]{1,0:T(8,128)}, f32[16,128]{1,0:T(8,128)}, f32[16,128]{1,0:T(8,128)}, f32[8,128]{1,0:T(8,128)}) custom-call(f32[16,128]{1,0:T(8,128)} %positions.1, f32[16,128]{1,0:T(8,128)} %velocities.1, f32[1,128]{1,0:T(1,128)} %bitcast.19, s32[1,128]{1,0:T(1,128)} %bitcast.20, f32[1,128]{1,0:T(1,128)} %bitcast.21, f32[1,128]{1,0:T(1,128)} %bitcast.22, ...), custom_call_target="tpu_custom_call" | custom-call | tf_op jit(solution)/shard_map/start/pallas_call | solution.py:251
  2.3 15.6 %all-to-all-start = ((f32[8,43,1,128]{3,2,1,0:T(1,128)}), f32[8,43,1,128]{3,2,1,0:T(1,128)S(1)}, u32[]{:S(2)}, u32[]{:S(2)}) async-start(f32[8,43,1,128]{3,2,1,0:T(1,128)} %bitcast.16), calls=%async_computation | async-start | bytes 352256 | tf_op jit(solution)/shard_map/all_to_all | solution.py:244
  17.9 0.8 reshape.50
  18.8 2.1 %reshape.52.waves = s32[4096,1]{1,0:T(8,128)S(1)} reshape(s32[16,8,32]{2,1,0:T(8,128)S(1)} %copy.18) | data formatting | bytes 32768 | tf_op jit(solution)/shard_map/reshape | solution.py:249
  20.9 11.8 %all-to-all-done = f32[8,43,1,128]{3,2,1,0:T(1,128)S(1)} async-done(((f32[8,43,1,128]{3,2,1,0:T(1,128)}), f32[8,43,1,128]{3,2,1,0:T(1,128)S(1)}, u32[]{:S(2)}, u32[]{:S(2)}) %all-to-all-start) | async-done | bytes 176160 | tf_op jit(solution)/shard_map/all_to_all | solution.py:244
  32.7 14.7 %first.1 = (bf16[4096,1024]{1,0:T(8,128)(2,1)S(1)}, bf16[4096,1024]{1,0:T(8,128)(2,1)S(1)}, f32[16,1024]{1,0:T(8,128)S(1)}, f32[1,1024]{1,0:T(1,128)S(1)}, f32[1...) custom-call(s32[1]{0:T(128)} %bitcast.place, ...), custom_call_target="tpu_custom_call" | custom-call | tf_op jit(solution)/shard_map/first/pallas_call | solution.py:255
  47.5 15.4 %all_to_all.25.received = f32[16,16,256]{2,1,0:T(8,128)S(1)} all-to-all(f32[16,16,256]{2,1,0:T(8,128)S(1)} %get-tuple-element.31), channel_id=1, replica_groups={{0,4,8,12,16,20,24,28,32,36,40,44,48,52,56,60},{64,68,72,76,80,84,88,92..., dimensions={0} | all-to-all | bytes 524288 | tf_op jit(solution)/shard_map/all_to_all | solution.py:244
  62.9 10.6 %all_to_all.26.received = f32[16,16,256]{2,1,0:T(8,128)S(1)} all-to-all(f32[16,16,256]{2,1,0:T(8,128)S(1)} %get-tuple-element.35), channel_id=1, replica_groups={{0,4,8,12,16,20,24,28,32,36,40,44,48,52,56,60},{64,68,72,76,80,84,88,92..., dimensions={0} | all-to-all | bytes 524288 | tf_op jit(solution)/shard_map/all_to_all | solution.py:244
  73.6 0.0 copy-start
  73.6 0.0 copy-start.1
  73.6 0.0 copy-start.2
  73.6 7.7 %middle.1 = (f32[16,128]{1,0:T(8,128)S(1)}, f32[16,16,256]{2,1,0:T(8,128)S(1)}) custom-call(s32[1]{0:T(128)} %get-tuple-element.30.place, f32[16,16,256]{2,1,0:T(8,128)S(1)} %all_to_all.26.received, f32[16,1024]{1,0:T(8,128)S(1)} %get-tuple-element.36.free_ref, f32[1,1024]{1,0:T(1,128)S(1)} %get-tuple-element.37.square_ref, ...), custom_call_target="tpu_custom_call" | custom-call | tf_op jit(solution)/shard_map/middle/pallas_call | solution.py:257
  81.3 10.6 %all_to_all.27.received = f32[16,16,256]{2,1,0:T(8,128)S(1)} all-to-all(f32[16,16,256]{2,1,0:T(8,128)S(1)} %get-tuple-element.40), channel_id=1, replica_groups={{0,4,8,12,16,20,24,28,32,36,40,44,48,52,56,60},{64,68,72,76,80,84,88,92..., dimensions={0} | all-to-all | bytes 524288 | tf_op jit(solution)/shard_map/all_to_all | solution.py:244
  92.0 10.6 %all_to_all.28.received = f32[16,16,256]{2,1,0:T(8,128)S(1)} all-to-all(f32[16,16,256]{2,1,0:T(8,128)S(1)} %get-tuple-element.43), channel_id=1, replica_groups={{0,4,8,12,16,20,24,28,32,36,40,44,48,52,56,60},{64,68,72,76,80,84,88,92..., dimensions={0} | all-to-all | bytes 524288 | tf_op jit(solution)/shard_map/all_to_all | solution.py:244
  102.6 0.0 copy-done
  102.6 0.0 copy-done.1
  102.6 0.0 copy-done.2
  102.6 2.1 %last.1 = (f32[16,128]{1,0:T(8,128)}, f32[16,128]{1,0:T(8,128)}, f32[16,32]{1,0:T(8,128)}, f32[16,32]{1,0:T(8,128)}) custom-call(s32[1]{0:T(128)} %get-tuple-element.30.place, f32[16,16,256]{2,1,0:T(8,128)S(1)} %all_to_all.28.received, bf16[4096,1024]{1,0:T(8,128)(2,1)S(1)} %get-tuple-element.38.high_ref, bf16[4096,1024]{1,0:T(8,128)(2,1)S(1)} %get-tuple-element.39.low_ref, ...), custom_call_target="tpu_custom_call" | custom-call | tf_op jit(solution)/shard_map/last/pallas_call | solution.py:259
  (3 shorter events, 0.1 us)
Async XLA Ops:
  2.3 30.5 %all-to-all-start = ((f32[8,43,1,128]{3,2,1,0:T(1,128)}), f32[8,43,1,128]{3,2,1,0:T(1,128)S(1)}, u32[]{:S(2)}, u32[]{:S(2)}) async-start(f32[8,43,1,128]{3,2,1,0:T(1,128)} %bitcast.16), calls=%async_computation | async-start | bytes 352256 | tf_op jit(solution)/shard_map/all_to_all | solution.py:244
  73.6 29.0 %copy-start = (f32[16,128]{1,0:T(8,128)S(1)}, f32[16,128]{1,0:T(8,128)}, u32[]{:S(2)}) copy-start(f32[16,128]{1,0:T(8,128)} %get-tuple-element.45.free_positions) | copy-start | bytes 24580
  73.6 29.0 %copy-start.1 = (f32[16,128]{1,0:T(8,128)S(1)}, f32[16,128]{1,0:T(8,128)}, u32[]{:S(2)}) copy-start(f32[16,128]{1,0:T(8,128)} %get-tuple-element.46.free_velocities) | copy-start | bytes 24580
  73.6 29.0 %copy-start.2 = (f32[8,128]{1,0:T(8,128)S(1)}, f32[8,128]{1,0:T(8,128)}, u32[]{:S(2)}) copy-start(f32[8,128]{1,0:T(8,128)} %get-tuple-element.47.bond_ref) | copy-start | bytes 12292

commit v6 on v5

--- a/solution.py
+++ b/solution.py
@@ -118,15 +118,14 @@
         taken = pl.ds(pl.multiple_of(member * chunk, chunk), chunk)
         wave = waves[taken, :]
         for q in range(sets):
-            columns = pl.ds(q * LANES, LANES)
             high, low = split(sine_of(wave * sites[q]))
-            high_ref[taken, columns] = high
-            low_ref[taken, columns] = low
-            held_high[slot, :, columns] = high
-            held_low[slot, :, columns] = low
+            high_ref[q, taken, :] = high
+            low_ref[q, taken, :] = low
+            held_high[slot, q] = high
+            held_low[slot, q] = low
 
     def finish(member, slot):
-        out_ref[member] = product(dipole_ref[...], held_high[slot], held_low[slot], 1)
+        out_ref[member] = product(dipole_ref[...], wide(held_high.at[slot]), wide(held_low.at[slot]), 1)
 
     def step(pair, carry):
         for slot in range(2):
@@ -154,18 +153,22 @@
         out_ref[member] = weighted
 
 
-def pull_of(received, high_ref, low_ref, columns):
+def wide(ref, rows=slice(None)):
+    return jnp.concatenate([ref[q, rows, :] for q in range(ref.shape[0])], axis=1)
+
+
+def pull_of(received, read_high, read_low):
     chunk = received.shape[2]
     pull = None
     for member in range(received.shape[0]):
         rows = pl.ds(member * chunk, chunk)
-        piece = product(both(received[member]), high_ref[rows, columns], low_ref[rows, columns], 0)
+        piece = product(both(received[member]), read_high(rows), read_low(rows), 0)
         pull = piece if pull is None else pull + piece
     return pull
 
 
 def middle_kernel(place, received, free_ref, square_ref, high_ref, low_ref, pull_out, out_ref):
-    pull = pull_of(received, high_ref, low_ref, slice(None))
+    pull = pull_of(received, functools.partial(wide, high_ref), functools.partial(wide, low_ref))
     own = pull[:, :LANES]
     for q in range(1, pull.shape[1] // LANES):
         own = jnp.where(place[0] == q, pull[:, q * LANES : (q + 1) * LANES], own)
@@ -174,7 +177,7 @@
     chunk = out_ref.shape[2]
     for member in range(out_ref.shape[0]):
         rows = pl.ds(member * chunk, chunk)
-        out_ref[member] = product(dipole, high_ref[rows, :], low_ref[rows, :], 1)
+        out_ref[member] = product(dipole, wide(high_ref, rows), wide(low_ref, rows), 1)
 
 
 def last_kernel(place, received, high_ref, low_ref, pull, free_positions, free_velocities, bond_ref, amplitudes, momenta,
@@ -185,8 +188,8 @@
         for q in range(1, whole.shape[1] // owned):
             mine = jnp.where(place[0] == q, whole[:, q * owned : (q + 1) * owned], mine)
         own[...] = mine
-    columns = pl.ds(pl.multiple_of(place[0] * LANES, LANES), LANES)
-    last_pull = pull_of(received, high_ref, low_ref, columns)
+    here = place[0]
+    last_pull = pull_of(received, lambda rows: high_ref[here, rows, :], lambda rows: low_ref[here, rows, :])
     slope, depth, stiffness = (bond_ref[i : i + 1, :] for i in range(3))
     first = slope * pull[...]
     velocities = free_velocities[...] - STEP_TIME * first
@@ -218,7 +221,7 @@
     f = lambda *shape: (shape, F32)
     held = [pltpu.VMEM(s, F32) for s in (bond, bond, row)] + [pltpu.VMEM(row, jnp.int32)]
     held += [pltpu.VMEM(s, F32) for s in (row, row, own, own, own_row, own_row)]
-    phase = ((modes, here), BF16)
+    phase = ((sets, modes, mols), BF16)
     state, blocks = f(traj, chunk), f(SET, traj, chunk)
     make = functools.partial(call, interpret=interpret)
     return dict(
@@ -226,7 +229,7 @@
                    held + [pltpu.SemaphoreType.DMA((len(held),))], grant=56),
         first=make(functools.partial(first_kernel, shift, traj),
                    [phase, phase, f(traj, here), f(1, here), state, state, f(2, chunk), ((1,), jnp.int32), blocks], "first", "SVV",
-                   [pltpu.VMEM((2 * traj, here), BF16)] + 2 * [pltpu.VMEM((2, chunk, here), BF16)]),
+                   [pltpu.VMEM((2 * traj, here), BF16)] + 2 * [pltpu.VMEM((2, sets, chunk, mols), BF16)]),
         modes=make(modes_kernel, [state, state, blocks], "modes", "VVVV"),
         middle=make(middle_kernel, [f(*bond), blocks], "middle", "SVVVVV"),
         last=make(last_kernel, [f(*bond), f(*bond), f(*own), f(*own)], "last", "S" + 9 * "V"),

time: 105 us -> 104 us (level)
  Pallas kernels: 26.2 us -> 24.6 us
    pallas_call x1, Pallas kernels: 14.7 us -> 13.3 us  [local(): run['first'](place, block, waves)]
where the time goes in v6:
time: 104 us; the launch traced here: 103 us
  blocking collectives  47.3 us (45%)
  Pallas kernels  24.6 us (24%)
  starting transfers between devices  15.6 us (15%)
  waiting for transfers between devices  11.8 us (11%)
  local copies, waits for them, and re-layouts  2.98 us (3%)
    all_to_all x4, blocking collectives, exchange(): lax.all_to_all(blocks, 'mol', 0, 0, axis_index_groups=groups, tiled=True)  47.3 us
    all_to_all x1, starting transfers between devices, exchange(): lax.all_to_all(blocks, 'mol', 0, 0, axis_index_groups=groups, tiled=True)  15.6 us
    pallas_call x1, Pallas kernels, local(): run['first'](place, block, waves)  13.3 us
    all_to_all x1, waiting for transfers between devices, exchange(): lax.all_to_all(blocks, 'mol', 0, 0, axis_index_groups=groups, tiled=True)  11.8 us
    pallas_call x1, Pallas kernels, local(): run['middle'](place, exchange(block, inside), free, square, high, low)  7.75 us
    reshape x2, local copies, waits for them, and re-layouts, local(): wavevectors.reshape(sets, SET, owned).transpose(1, 0, 2).reshape(-1, 1)  2.94 us
  transfers between devices with their start and end apart: 1, of which 1 were waited for; matrix products, arithmetic and copies ran while one was open for 3% of the time, Pallas kernels for 0%

profile of v6, /device:TPU:1, one launch (start us, length us, event | category | flops | bytes accessed | tf_op | source)
XLA Modules:
  0.0 103.1 jit_solution(5617194157699948177)
XLA Ops:
  0.6 1.7 %start.1 = (f32[344,128]{1,0:T(8,128)}, f32[16,128]{1,0:T(8,128)}, f32[16,128]{1,0:T(8,128)}, f32[8,128]{1,0:T(8,128)}) custom-call(f32[16,128]{1,0:T(8,128)} %positions.1, f32[16,128]{1,0:T(8,128)} %velocities.1, f32[1,128]{1,0:T(1,128)} %bitcast.19, s32[1,128]{1,0:T(1,128)} %bitcast.20, f32[1,128]{1,0:T(1,128)} %bitcast.21, f32[1,128]{1,0:T(1,128)} %bitcast.22, ...), custom_call_target="tpu_custom_call" | custom-call | tf_op jit(solution)/shard_map/start/pallas_call | solution.py:254
  2.3 15.6 %all-to-all-start = ((f32[8,43,1,128]{3,2,1,0:T(1,128)}), f32[8,43,1,128]{3,2,1,0:T(1,128)S(1)}, u32[]{:S(2)}, u32[]{:S(2)}) async-start(f32[8,43,1,128]{3,2,1,0:T(1,128)} %bitcast.16), calls=%async_computation | async-start | bytes 352256 | tf_op jit(solution)/shard_map/all_to_all | solution.py:247
  17.9 0.8 reshape.50
  18.8 2.1 %reshape.52.waves = s32[4096,1]{1,0:T(8,128)S(1)} reshape(s32[16,8,32]{2,1,0:T(8,128)S(1)} %copy.18) | data formatting | bytes 32768 | tf_op jit(solution)/shard_map/reshape | solution.py:252
  20.9 11.8 %all-to-all-done = f32[8,43,1,128]{3,2,1,0:T(1,128)S(1)} async-done(((f32[8,43,1,128]{3,2,1,0:T(1,128)}), f32[8,43,1,128]{3,2,1,0:T(1,128)S(1)}, u32[]{:S(2)}, u32[]{:S(2)}) %all-to-all-start) | async-done | bytes 176160 | tf_op jit(solution)/shard_map/all_to_all | solution.py:247
  32.7 13.3 %first.1 = (bf16[8,4096,128]{2,1,0:T(8,128)(2,1)S(1)}, bf16[8,4096,128]{2,1,0:T(8,128)(2,1)S(1)}, f32[16,1024]{1,0:T(8,128)S(1)}, f32[1,1024]{1,0:T(1,128)S(1)},...) custom-call(s32[1]{0:T(128)} %bitcast.place, ...), custom_call_target="tpu_custom_call" | custom-call | tf_op jit(solution)/shard_map/first/pallas_call | solution.py:258
  46.1 15.4 %all_to_all.25.received = f32[16,16,256]{2,1,0:T(8,128)S(1)} all-to-all(f32[16,16,256]{2,1,0:T(8,128)S(1)} %get-tuple-element.31), channel_id=1, replica_groups={{0,4,8,12,16,20,24,28,32,36,40,44,48,52,56,60},{64,68,72,76,80,84,88,92..., dimensions={0} | all-to-all | bytes 524288 | tf_op jit(solution)/shard_map/all_to_all | solution.py:247
  61.6 10.6 %all_to_all.26.received = f32[16,16,256]{2,1,0:T(8,128)S(1)} all-to-all(f32[16,16,256]{2,1,0:T(8,128)S(1)} %get-tuple-element.35), channel_id=1, replica_groups={{0,4,8,12,16,20,24,28,32,36,40,44,48,52,56,60},{64,68,72,76,80,84,88,92..., dimensions={0} | all-to-all | bytes 524288 | tf_op jit(solution)/shard_map/all_to_all | solution.py:247
  72.2 0.0 copy-start
  72.2 0.0 copy-start.1
  72.2 0.0 copy-start.2
  72.2 7.8 %middle.1 = (f32[16,128]{1,0:T(8,128)S(1)}, f32[16,16,256]{2,1,0:T(8,128)S(1)}) custom-call(s32[1]{0:T(128)} %get-tuple-element.30.place, f32[16,16,256]{2,1,0:T(8,128)S(1)} %all_to_all.26.received, f32[16,1024]{1,0:T(8,128)S(1)} %get-tuple-element.36.free_ref, f32[1,1024]{1,0:T(1,128)S(1)} %get-tuple-element.37.square_ref, ...), custom_call_target="tpu_custom_call" | custom-call | tf_op jit(solution)/shard_map/middle/pallas_call | solution.py:260
  80.0 10.6 %all_to_all.27.received = f32[16,16,256]{2,1,0:T(8,128)S(1)} all-to-all(f32[16,16,256]{2,1,0:T(8,128)S(1)} %get-tuple-element.40), channel_id=1, replica_groups={{0,4,8,12,16,20,24,28,32,36,40,44,48,52,56,60},{64,68,72,76,80,84,88,92..., dimensions={0} | all-to-all | bytes 524288 | tf_op jit(solution)/shard_map/all_to_all | solution.py:247
  90.6 10.6 %all_to_all.28.received = f32[16,16,256]{2,1,0:T(8,128)S(1)} all-to-all(f32[16,16,256]{2,1,0:T(8,128)S(1)} %get-tuple-element.43), channel_id=1, replica_groups={{0,4,8,12,16,20,24,28,32,36,40,44,48,52,56,60},{64,68,72,76,80,84,88,92..., dimensions={0} | all-to-all | bytes 524288 | tf_op jit(solution)/shard_map/all_to_all | solution.py:247
  101.3 0.0 copy-done
  101.3 0.0 copy-done.1
  101.3 0.0 copy-done.2
  101.3 1.8 %last.1 = (f32[16,128]{1,0:T(8,128)}, f32[16,128]{1,0:T(8,128)}, f32[16,32]{1,0:T(8,128)}, f32[16,32]{1,0:T(8,128)}) custom-call(s32[1]{0:T(128)} %get-tuple-element.30.place, f32[16,16,256]{2,1,0:T(8,128)S(1)} %all_to_all.28.received, bf16[8,4096,128]{2,1,0:T(8,128)(2,1)S(1)} %get-tuple-element.38.high_ref, ...), custom_call_target="tpu_custom_call" | custom-call | tf_op jit(solution)/shard_map/last/pallas_call | solution.py:262
  (3 shorter events, 0.1 us)
Async XLA Ops:
  2.3 30.5 %all-to-all-start = ((f32[8,43,1,128]{3,2,1,0:T(1,128)}), f32[8,43,1,128]{3,2,1,0:T(1,128)S(1)}, u32[]{:S(2)}, u32[]{:S(2)}) async-start(f32[8,43,1,128]{3,2,1,0:T(1,128)} %bitcast.16), calls=%async_computation | async-start | bytes 352256 | tf_op jit(solution)/shard_map/all_to_all | solution.py:247
  72.2 29.1 %copy-start = (f32[16,128]{1,0:T(8,128)S(1)}, f32[16,128]{1,0:T(8,128)}, u32[]{:S(2)}) copy-start(f32[16,128]{1,0:T(8,128)} %get-tuple-element.45.free_positions) | copy-start | bytes 24580
  72.2 29.1 %copy-start.1 = (f32[16,128]{1,0:T(8,128)S(1)}, f32[16,128]{1,0:T(8,128)}, u32[]{:S(2)}) copy-start(f32[16,128]{1,0:T(8,128)} %get-tuple-element.46.free_velocities) | copy-start | bytes 24580
  72.2 29.1 %copy-start.2 = (f32[8,128]{1,0:T(8,128)S(1)}, f32[8,128]{1,0:T(8,128)}, u32[]{:S(2)}) copy-start(f32[8,128]{1,0:T(8,128)} %get-tuple-element.47.bond_ref) | copy-start | bytes 12292

commit v7 on v6

--- a/solution.py
+++ b/solution.py
@@ -9,7 +9,9 @@
 
 STEP_TIME = 0.2
 SET = 16
-SINE = (25.13273048400879, -64.83467864990234, 67.04389953613281, -38.12319564819336, 12.233302116394043)
+SINE = (12.695119857788086, -20.77156639099121, 13.623412132263184, -4.913383483886719)
+SCALE = 1.2556471824645996
+QUARTER = 0.39416247606277466
 F32, BF16 = jnp.float32, jnp.bfloat16
 SUB = 8
 LANES = 128
@@ -35,12 +37,12 @@
 
 
 def sine_of(product):
-    turn = product.astype(F32) * (2.0**-32)
+    turn = product.astype(F32) * (SCALE * 2.0**-32)
     square = turn * turn
-    value = square * SINE[-1] + SINE[-2]
-    for factor in SINE[-3::-1]:
+    value = square + SINE[-1]
+    for factor in SINE[-2::-1]:
         value = value * square + factor
-    return turn * (0.25 - square) * value
+    return turn * (QUARTER - square) * value
 
 
 def morse(positions, depth, stiffness):

time: 104 us -> 103 us (level)
  no operation moved by 1% of the time
where the time goes in v7:
time: 103 us
  blocking collectives  47.3 us (46%)
  Pallas kernels  24.1 us (23%)
  starting transfers between devices  15.6 us (15%)
  waiting for transfers between devices  11.8 us (11%)
  local copies, waits for them, and re-layouts  2.98 us (3%)
    all_to_all x4, blocking collectives, exchange(): lax.all_to_all(blocks, 'mol', 0, 0, axis_index_groups=groups, tiled=True)  47.3 us
    all_to_all x1, starting transfers between devices, exchange(): lax.all_to_all(blocks, 'mol', 0, 0, axis_index_groups=groups, tiled=True)  15.6 us
    pallas_call x1, Pallas kernels, local(): run['first'](place, block, waves)  12.8 us
    all_to_all x1, waiting for transfers between devices, exchange(): lax.all_to_all(blocks, 'mol', 0, 0, axis_index_groups=groups, tiled=True)  11.8 us
    pallas_call x1, Pallas kernels, local(): run['middle'](place, exchange(block, inside), free, square, high, low)  7.75 us
    reshape x2, local copies, waits for them, and re-layouts, local(): wavevectors.reshape(sets, SET, owned).transpose(1, 0, 2).reshape(-1, 1)  2.94 us
  transfers between devices with their start and end apart: 1, of which 1 were waited for; matrix products, arithmetic and copies ran while one was open for 3% of the time, Pallas kernels for 0%

profile of v7, /device:TPU:1, one launch (start us, length us, event | category | flops | bytes accessed | tf_op | source)
XLA Modules:
  0.0 102.5 jit_solution(961657293296105586)
XLA Ops:
  0.6 1.7 %start.1 = (f32[344,128]{1,0:T(8,128)}, f32[16,128]{1,0:T(8,128)}, f32[16,128]{1,0:T(8,128)}, f32[8,128]{1,0:T(8,128)}) custom-call(f32[16,128]{1,0:T(8,128)} %positions.1, f32[16,128]{1,0:T(8,128)} %velocities.1, f32[1,128]{1,0:T(1,128)} %bitcast.19, s32[1,128]{1,0:T(1,128)} %bitcast.20, f32[1,128]{1,0:T(1,128)} %bitcast.21, f32[1,128]{1,0:T(1,128)} %bitcast.22, ...), custom_call_target="tpu_custom_call" | custom-call | tf_op jit(solution)/shard_map/start/pallas_call | solution.py:256
  2.3 15.6 %all-to-all-start = ((f32[8,43,1,128]{3,2,1,0:T(1,128)}), f32[8,43,1,128]{3,2,1,0:T(1,128)S(1)}, u32[]{:S(2)}, u32[]{:S(2)}) async-start(f32[8,43,1,128]{3,2,1,0:T(1,128)} %bitcast.16), calls=%async_computation | async-start | bytes 352256 | tf_op jit(solution)/shard_map/all_to_all | solution.py:249
  17.9 0.8 reshape.50
  18.8 2.1 %reshape.52.waves = s32[4096,1]{1,0:T(8,128)S(1)} reshape(s32[16,8,32]{2,1,0:T(8,128)S(1)} %copy.18) | data formatting | bytes 32768 | tf_op jit(solution)/shard_map/reshape | solution.py:254
  20.9 11.8 %all-to-all-done = f32[8,43,1,128]{3,2,1,0:T(1,128)S(1)} async-done(((f32[8,43,1,128]{3,2,1,0:T(1,128)}), f32[8,43,1,128]{3,2,1,0:T(1,128)S(1)}, u32[]{:S(2)}, u32[]{:S(2)}) %all-to-all-start) | async-done | bytes 176160 | tf_op jit(solution)/shard_map/all_to_all | solution.py:249
  32.7 12.8 %first.1 = (bf16[8,4096,128]{2,1,0:T(8,128)(2,1)S(1)}, bf16[8,4096,128]{2,1,0:T(8,128)(2,1)S(1)}, f32[16,1024]{1,0:T(8,128)S(1)}, f32[1,1024]{1,0:T(1,128)S(1)},...) custom-call(s32[1]{0:T(128)} %bitcast.place, ...), custom_call_target="tpu_custom_call" | custom-call | tf_op jit(solution)/shard_map/first/pallas_call | solution.py:260
  45.6 15.4 %all_to_all.25.received = f32[16,16,256]{2,1,0:T(8,128)S(1)} all-to-all(f32[16,16,256]{2,1,0:T(8,128)S(1)} %get-tuple-element.31), channel_id=1, replica_groups={{0,4,8,12,16,20,24,28,32,36,40,44,48,52,56,60},{64,68,72,76,80,84,88,92..., dimensions={0} | all-to-all | bytes 524288 | tf_op jit(solution)/shard_map/all_to_all | solution.py:249
  61.1 10.6 %all_to_all.26.received = f32[16,16,256]{2,1,0:T(8,128)S(1)} all-to-all(f32[16,16,256]{2,1,0:T(8,128)S(1)} %get-tuple-element.35), channel_id=1, replica_groups={{0,4,8,12,16,20,24,28,32,36,40,44,48,52,56,60},{64,68,72,76,80,84,88,92..., dimensions={0} | all-to-all | bytes 524288 | tf_op jit(solution)/shard_map/all_to_all | solution.py:249
  71.7 0.0 copy-start
  71.7 0.0 copy-start.1
  71.7 0.0 copy-start.2
  71.7 7.8 %middle.1 = (f32[16,128]{1,0:T(8,128)S(1)}, f32[16,16,256]{2,1,0:T(8,128)S(1)}) custom-call(s32[1]{0:T(128)} %get-tuple-element.30.place, f32[16,16,256]{2,1,0:T(8,128)S(1)} %all_to_all.26.received, f32[16,1024]{1,0:T(8,128)S(1)} %get-tuple-element.36.free_ref, f32[1,1024]{1,0:T(1,128)S(1)} %get-tuple-element.37.square_ref, ...), custom_call_target="tpu_custom_call" | custom-call | tf_op jit(solution)/shard_map/middle/pallas_call | solution.py:262
  79.4 10.6 %all_to_all.27.received = f32[16,16,256]{2,1,0:T(8,128)S(1)} all-to-all(f32[16,16,256]{2,1,0:T(8,128)S(1)} %get-tuple-element.40), channel_id=1, replica_groups={{0,4,8,12,16,20,24,28,32,36,40,44,48,52,56,60},{64,68,72,76,80,84,88,92..., dimensions={0} | all-to-all | bytes 524288 | tf_op jit(solution)/shard_map/all_to_all | solution.py:249
  90.1 10.6 %all_to_all.28.received = f32[16,16,256]{2,1,0:T(8,128)S(1)} all-to-all(f32[16,16,256]{2,1,0:T(8,128)S(1)} %get-tuple-element.43), channel_id=1, replica_groups={{0,4,8,12,16,20,24,28,32,36,40,44,48,52,56,60},{64,68,72,76,80,84,88,92..., dimensions={0} | all-to-all | bytes 524288 | tf_op jit(solution)/shard_map/all_to_all | solution.py:249
  100.7 0.0 copy-done
  100.7 0.0 copy-done.1
  100.7 0.0 copy-done.2
  100.8 1.8 %last.1 = (f32[16,128]{1,0:T(8,128)}, f32[16,128]{1,0:T(8,128)}, f32[16,32]{1,0:T(8,128)}, f32[16,32]{1,0:T(8,128)}) custom-call(s32[1]{0:T(128)} %get-tuple-element.30.place, f32[16,16,256]{2,1,0:T(8,128)S(1)} %all_to_all.28.received, bf16[8,4096,128]{2,1,0:T(8,128)(2,1)S(1)} %get-tuple-element.38.high_ref, ...), custom_call_target="tpu_custom_call" | custom-call | tf_op jit(solution)/shard_map/last/pallas_call | solution.py:264
  (3 shorter events, 0.1 us)
Async XLA Ops:
  2.3 30.5 %all-to-all-start = ((f32[8,43,1,128]{3,2,1,0:T(1,128)}), f32[8,43,1,128]{3,2,1,0:T(1,128)S(1)}, u32[]{:S(2)}, u32[]{:S(2)}) async-start(f32[8,43,1,128]{3,2,1,0:T(1,128)} %bitcast.16), calls=%async_computation | async-start | bytes 352256 | tf_op jit(solution)/shard_map/all_to_all | solution.py:249
  71.7 29.1 %copy-start = (f32[16,128]{1,0:T(8,128)S(1)}, f32[16,128]{1,0:T(8,128)}, u32[]{:S(2)}) copy-start(f32[16,128]{1,0:T(8,128)} %get-tuple-element.45.free_positions) | copy-start | bytes 24580
  71.7 29.1 %copy-start.1 = (f32[16,128]{1,0:T(8,128)S(1)}, f32[16,128]{1,0:T(8,128)}, u32[]{:S(2)}) copy-start(f32[16,128]{1,0:T(8,128)} %get-tuple-element.46.free_velocities) | copy-start | bytes 24580
  71.7 29.1 %copy-start.2 = (f32[8,128]{1,0:T(8,128)S(1)}, f32[8,128]{1,0:T(8,128)}, u32[]{:S(2)}) copy-start(f32[8,128]{1,0:T(8,128)} %get-tuple-element.47.bond_ref) | copy-start | bytes 12292
